TPU v7x, 128 devices: a whole 4x4x4 slice. The times are simulated.
128 devices in a mesh: seq: 8 (over y, x_lo), fsdp: 16 (over z, x_hi, core).
Axes of the slice: x: 4 (x_hi: 2, x_lo: 2; x = x_hi * 2 + x_lo), y: 4, z: 4, core: 2. Of those that a mesh axis runs over, the one named last changes fastest.
Arguments:
- hidden_in: bfloat16 [16, 2048, 1024], P('fsdp', 'seq'), may hold values from -40 to 40
- norm_gain: bfloat16 [1024], P('fsdp'), may hold values from 0.5 to 1.5
- mixer_proj: bfloat16 [1024, 3352], P('fsdp'), may hold values from -0.1875 to 0.1875
- attn_proj: bfloat16 [1024, 768], P('fsdp'), may hold values from -8 to 8
- conv_kernel: bfloat16 [1792, 4], P('fsdp'), may hold values from -1.5 to 1.5
- conv_bias: bfloat16 [1792], P('fsdp'), may hold values from -1.5 to 1.5
- step_bias: float32 [24], replicated, may hold values from -4.6 to -2.3
- decay_log: float32 [24], replicated, may hold values from 0 to 2.77
- skip_gain: float32 [24], replicated, may hold values from 0.5 to 2
- gated_gain: bfloat16 [1536], P('fsdp'), may hold values from 0.5 to 1.5
- mixer_out: bfloat16 [1536, 1024], P('fsdp'), may hold values from -0.15625 to 0.15625
- attn_out: bfloat16 [512, 1024], P('fsdp'), may hold values from -0.75 to 0.75
- ffn_gain: bfloat16 [1024], P('fsdp'), may hold values from 0.5 to 1.5
- gate_up: bfloat16 [1024, 4096], P('fsdp'), may hold values from -0.1875 to 0.1875
- down_proj: bfloat16 [2048, 1024], P('fsdp'), may hold values from -0.125 to 0.125
- out_grad: bfloat16 [16, 2048, 1024], P('fsdp', 'seq'), may hold values from -6 to 6
Outputs:
- block_out: bfloat16 [16, 2048, 1024], P('fsdp', 'seq')
- input_grad: float32 [16, 2048, 1024], P('fsdp', 'seq')
- grad_norm: float32 [1024], P('fsdp')
- grad_mixer: float32 [1024, 3352], P('fsdp')
- grad_attn: float32 [1024, 768], P('fsdp')
- grad_kernel: float32 [1792, 4], P('fsdp')
- grad_convbias: float32 [1792], P('fsdp')
- grad_step: float32 [24], replicated
- grad_decay: float32 [24], replicated
- grad_skip: float32 [24], replicated
- grad_gated: float32 [1536], P('fsdp')
- grad_mixed: float32 [1536, 1024], P('fsdp')
- grad_attended: float32 [512, 1024], P('fsdp')
- grad_ffn: float32 [1024], P('fsdp')
- grad_gateup: float32 [1024, 4096], P('fsdp')
- grad_down: float32 [2048, 1024], P('fsdp')
All inputs are finite; a program needn't handle non-finite values.
Results may differ from a plain program's by a relative error of at most 0.024.
Values may be sent and summed in bfloat16 or wider, within the bound.
A program may use at most 192 MiB of HBM per device.

v0:
```python
import math

import jax
import jax.numpy as jnp
from jax import lax
from jax.sharding import PartitionSpec as P

MH = 24
NST = 128
QH = 8
KVH = 2
AP = 64
FF = 2048
STRETCH = 256
D_SSM = 1536


EPSILON = 1e-05
THETA = 10000.0
HIGHEST = lax.Precision.HIGHEST


def silu_slope(value):
    sigma = jax.nn.sigmoid(value)
    return sigma * (1.0 + value * (1.0 - sigma))


def rms_scale(value):
    return lax.rsqrt(jnp.mean(value * value, axis=1, keepdims=True) + EPSILON)


def rms_back(grad_normed, normed, scale):
    return scale * (grad_normed - normed * jnp.mean(grad_normed * normed, axis=1, keepdims=True))


def rope_tables(length, width):
    half = width // 2
    inverse = THETA ** (-2.0 * jnp.arange(half).astype(jnp.float32) / width)
    angles = jnp.arange(length).astype(jnp.float32)[:, None] * inverse[None, :]
    return (jnp.cos(angles), jnp.sin(angles))


def rotate(value, cosine, sine):
    half = value.shape[-1] // 2
    first = value[..., :half]
    second = value[..., half:]
    return jnp.concatenate(
        [first * cosine - second * sine, second * cosine + first * sine], axis=-1
    )


def unrotate(grad, cosine, sine):
    half = grad.shape[-1] // 2
    first = grad[..., :half]
    second = grad[..., half:]
    return jnp.concatenate(
        [first * cosine + second * sine, second * cosine - first * sine], axis=-1
    )


def conv_apply(signal, kernel, offset):
    length = signal.shape[0]
    taps = kernel.shape[1]
    padded = jnp.pad(signal, ((taps - 1, 0), (0, 0)))
    result = offset[None, :] + jnp.zeros_like(signal)
    for lag in range(taps):
        result = result + kernel[:, lag][None, :] * padded[lag : lag + length]
    return result


def ssd_scan(xinput, delta, decay, bmatrix, cmatrix, skip):
    length, heads, width = xinput.shape
    nstate = bmatrix.shape[1]
    count = length // STRETCH
    xblocks = xinput.reshape(count, STRETCH, heads, width)
    dblocks = delta.reshape(count, STRETCH, heads)
    bblocks = bmatrix.reshape(count, STRETCH, nstate)
    cblocks = cmatrix.reshape(count, STRETCH, nstate)
    cumul = jnp.cumsum(dblocks * decay[None, None, :], axis=1)
    places = jnp.arange(STRETCH)
    lower = places[:, None] >= places[None, :]
    spread = cumul[:, :, None, :] - cumul[:, None, :, :]
    fading = jnp.exp(jnp.where(lower[None, :, :, None], spread, -jnp.inf))
    inner = jnp.einsum("cin,cjn->cij", cblocks, bblocks, precision=HIGHEST)
    mixing = inner[..., None] * fading * dblocks[:, None, :, :]
    y_inner = jnp.einsum("cijh,cjhp->cihp", mixing, xblocks, precision=HIGHEST)
    tails = jnp.exp(cumul[:, -1:, :] - cumul) * dblocks
    fresh = jnp.einsum("cjn,cjh,cjhp->chpn", bblocks, tails, xblocks, precision=HIGHEST)
    totals = jnp.exp(cumul[:, -1, :])

    def advance(state, pair):
        fade, added = pair
        return (fade[:, None, None] * state + added, state)

    _, starts = lax.scan(advance, jnp.zeros((heads, width, nstate), xinput.dtype), (totals, fresh))
    y_outer = (
        jnp.einsum("cin,chpn->cihp", cblocks, starts, precision=HIGHEST) * jnp.exp(cumul)[..., None]
    )
    output = y_inner + y_outer + skip[None, None, :, None] * xblocks
    return output.reshape(length, heads, width)


def mamba_heads(
    xpart, bcpart, kernel_x, kernel_bc, bias_x, bias_bc, steps_raw, step_bias, decay_log, skip_gain
):
    heads = steps_raw.shape[1]
    length = xpart.shape[0]
    nstate = bcpart.shape[1] // 2
    conv_x = jax.nn.silu(conv_apply(xpart, kernel_x, bias_x))
    conv_bc = jax.nn.silu(conv_apply(bcpart, kernel_bc, bias_bc))
    delta = jax.nn.softplus(steps_raw + step_bias[None, :])
    decay = -jnp.exp(decay_log)
    output = ssd_scan(
        conv_x.reshape(length, heads, -1),
        delta,
        decay,
        conv_bc[:, :nstate],
        conv_bc[:, nstate:],
        skip_gain,
    )
    return output.reshape(length, -1)


def attend(query, keys, values, qpos, kpos, scale):
    scores = jnp.dot(query, keys.T, preferred_element_type=jnp.float32) * scale
    scores = jnp.where(kpos[None, :] <= qpos[:, None], scores, -jnp.inf)
    top = jnp.max(scores, axis=1, keepdims=True)
    expo = jnp.exp(scores - top)
    total = jnp.sum(expo, axis=1, keepdims=True)
    probs = (expo / total).astype(jnp.bfloat16)
    output = jnp.dot(probs, values, preferred_element_type=jnp.float32).astype(jnp.bfloat16)
    return (output, (top + jnp.log(total))[:, 0])


def attend_back(query, keys, values, output, logsum, grad_out, qpos, kpos, scale):
    scores = jnp.dot(query, keys.T, preferred_element_type=jnp.float32) * scale
    scores = jnp.where(kpos[None, :] <= qpos[:, None], scores, -jnp.inf)
    probs = jnp.exp(scores - logsum[:, None])
    grad_values = jnp.dot(
        probs.astype(jnp.bfloat16).T, grad_out, preferred_element_type=jnp.float32
    )
    grad_probs = jnp.dot(grad_out, values.T, preferred_element_type=jnp.float32)
    centre = jnp.sum(
        grad_out.astype(jnp.float32) * output.astype(jnp.float32), axis=1, keepdims=True
    )
    grad_scores = (probs * (grad_probs - centre)).astype(jnp.bfloat16)
    grad_query = jnp.dot(grad_scores, keys, preferred_element_type=jnp.float32) * scale
    grad_keys = jnp.dot(grad_scores.T, query, preferred_element_type=jnp.float32) * scale
    return (grad_query, grad_keys, grad_values)


def token_front(hidden, norm_gain, mixer_proj, attn_proj):
    resid = hidden.astype(jnp.float32)
    scale_one = rms_scale(resid)
    normed_one = resid * scale_one
    normed_in = (normed_one * norm_gain.astype(jnp.float32)).astype(jnp.bfloat16)
    projection = jnp.dot(normed_in, mixer_proj, preferred_element_type=jnp.float32)
    gate_pre = projection[:, :D_SSM]
    xpart = projection[:, D_SSM : 2 * D_SSM].astype(jnp.bfloat16)
    bcpart = projection[:, 2 * D_SSM : 2 * D_SSM + 2 * NST].astype(jnp.bfloat16)
    steps_raw = projection[:, 2 * D_SSM + 2 * NST :].astype(jnp.bfloat16)
    attend_pre = jnp.dot(normed_in, attn_proj, preferred_element_type=jnp.float32)
    queries = attend_pre[:, : QH * AP].astype(jnp.bfloat16)
    keyvals = attend_pre[:, QH * AP :].astype(jnp.bfloat16)
    return (
        resid,
        scale_one,
        normed_one,
        normed_in,
        gate_pre,
        xpart,
        bcpart,
        steps_raw,
        queries,
        keyvals,
    )


def token_tail(
    resid,
    mixed_y,
    attn_tok,
    gate_pre,
    gated_gain,
    mixer_out,
    attn_out,
    ffn_gain,
    gate_up,
    down_proj,
):
    gated = mixed_y.astype(jnp.float32) * jax.nn.silu(gate_pre)
    scale_two = rms_scale(gated)
    normed_two = gated * scale_two
    normed_mix = (normed_two * gated_gain.astype(jnp.float32)).astype(jnp.bfloat16)
    branch = jnp.dot(normed_mix, mixer_out, preferred_element_type=jnp.float32)
    branch = branch + jnp.dot(attn_tok, attn_out, preferred_element_type=jnp.float32)
    middle = resid + branch
    scale_three = rms_scale(middle)
    normed_three = middle * scale_three
    normed_ffn = (normed_three * ffn_gain.astype(jnp.float32)).astype(jnp.bfloat16)
    gates = jnp.dot(normed_ffn, gate_up, preferred_element_type=jnp.float32)
    gate_half = gates[:, :FF]
    up_half = gates[:, FF:]
    activ = (jax.nn.silu(gate_half) * up_half).astype(jnp.bfloat16)
    block_out = (middle + jnp.dot(activ, down_proj, preferred_element_type=jnp.float32)).astype(
        jnp.bfloat16
    )
    saved = (
        scale_two,
        normed_two,
        normed_mix,
        scale_three,
        normed_three,
        normed_ffn,
        gate_half,
        up_half,
        activ,
    )
    return (block_out, saved)


def token_back_tail(
    out_grad,
    saved,
    mixed_y,
    attn_tok,
    gate_pre,
    gated_gain,
    mixer_out,
    attn_out,
    ffn_gain,
    gate_up,
    down_proj,
    layout,
):
    (
        scale_two,
        normed_two,
        normed_mix,
        scale_three,
        normed_three,
        normed_ffn,
        gate_half,
        up_half,
        activ,
    ) = saved
    grad_activ = jnp.dot(out_grad, down_proj.T, preferred_element_type=jnp.float32)
    grad_down = jnp.dot(layout(activ, 1).T, out_grad, preferred_element_type=jnp.float32)
    grad_gates = jnp.concatenate(
        [grad_activ * up_half * silu_slope(gate_half), grad_activ * jax.nn.silu(gate_half)], axis=1
    ).astype(jnp.bfloat16)
    grad_gateup = jnp.dot(layout(normed_ffn, 1).T, grad_gates, preferred_element_type=jnp.float32)
    grad_nffn = jnp.dot(grad_gates, gate_up.T, preferred_element_type=jnp.float32)
    grad_ffn = jnp.sum(grad_nffn * normed_three, axis=0)
    grad_middle = out_grad.astype(jnp.float32) + rms_back(
        grad_nffn * ffn_gain.astype(jnp.float32), normed_three, scale_three
    )
    middle_bf = grad_middle.astype(jnp.bfloat16)
    grad_mixed = jnp.dot(layout(normed_mix, 1).T, middle_bf, preferred_element_type=jnp.float32)
    grad_attended = jnp.dot(layout(attn_tok, 1).T, middle_bf, preferred_element_type=jnp.float32)
    grad_nmix = jnp.dot(middle_bf, mixer_out.T, preferred_element_type=jnp.float32)
    grad_otok = jnp.dot(middle_bf, attn_out.T, preferred_element_type=jnp.float32).astype(
        jnp.bfloat16
    )
    grad_gated = jnp.sum(grad_nmix * normed_two, axis=0)
    grad_gz = rms_back(grad_nmix * gated_gain.astype(jnp.float32), normed_two, scale_two)
    grad_ymix = (grad_gz * jax.nn.silu(gate_pre)).astype(jnp.bfloat16)
    grad_gate = grad_gz * mixed_y.astype(jnp.float32) * silu_slope(gate_pre)
    late = (grad_gated, grad_mixed, grad_attended, grad_ffn, grad_gateup, grad_down)
    return (grad_middle, grad_ymix, grad_otok, grad_gate, late)


def token_back_front(
    grad_middle,
    grad_gate,
    xgrad,
    bcgrad,
    stepgrad,
    qgrad,
    kvgrad,
    normed_in,
    normed_one,
    scale_one,
    norm_gain,
    mixer_proj,
    attn_proj,
    layout,
):
    grad_proj = jnp.concatenate(
        [grad_gate.astype(jnp.bfloat16), xgrad, bcgrad.astype(jnp.bfloat16), stepgrad], axis=1
    )
    grad_aproj = jnp.concatenate([qgrad, kvgrad.astype(jnp.bfloat16)], axis=1)
    ordered = layout(normed_in, 1).T
    grad_mixer = jnp.dot(ordered, grad_proj, preferred_element_type=jnp.float32)
    grad_attn = jnp.dot(ordered, grad_aproj, preferred_element_type=jnp.float32)
    grad_nin = jnp.dot(grad_proj, mixer_proj.T, preferred_element_type=jnp.float32)
    grad_nin = grad_nin + jnp.dot(grad_aproj, attn_proj.T, preferred_element_type=jnp.float32)
    grad_norm = jnp.sum(grad_nin * normed_one, axis=0)
    input_grad = grad_middle + rms_back(
        grad_nin * norm_gain.astype(jnp.float32), normed_one, scale_one
    )
    return (input_grad, grad_norm, grad_mixer, grad_attn)


def per_device(
    hidden_in,
    norm_gain,
    mixer_proj,
    attn_proj,
    conv_kernel,
    conv_bias,
    step_bias,
    decay_log,
    skip_gain,
    gated_gain,
    mixer_out,
    attn_out,
    ffn_gain,
    gate_up,
    down_proj,
    out_grad,
):
    shards = (
        norm_gain,
        mixer_proj,
        attn_proj,
        conv_kernel,
        conv_bias,
        gated_gain,
        mixer_out,
        attn_out,
        ffn_gain,
        gate_up,
        down_proj,
    )
    weights = (
        lax.all_gather(shards[0], "fsdp", axis=0, tiled=True),
        lax.all_gather(shards[1], "fsdp", axis=0, tiled=True),
        lax.all_gather(shards[2], "fsdp", axis=0, tiled=True),
        lax.all_gather(shards[3], "fsdp", axis=0, tiled=True),
        lax.all_gather(shards[4], "fsdp", axis=0, tiled=True),
        lax.all_gather(shards[5], "fsdp", axis=0, tiled=True),
        lax.all_gather(shards[6], "fsdp", axis=0, tiled=True),
        lax.all_gather(shards[7], "fsdp", axis=0, tiled=True),
        lax.all_gather(shards[8], "fsdp", axis=0, tiled=True),
        lax.all_gather(shards[9], "fsdp", axis=0, tiled=True),
        lax.all_gather(shards[10], "fsdp", axis=0, tiled=True),
    )
    (
        gain_one,
        proj_mixer,
        proj_attn,
        kernel_all,
        bias_all,
        gain_gated,
        out_mixer,
        out_attn,
        gain_ffn,
        proj_gateup,
        proj_down,
    ) = weights
    front = token_front(hidden_in[0], gain_one, proj_mixer, proj_attn)
    (
        resid,
        scale_one,
        normed_one,
        normed_in,
        gate_pre,
        xpart,
        bcpart,
        steps_raw,
        queries,
        keyvals,
    ) = front
    xheads, stepheads, qheads = (
        lax.all_to_all(xpart, "seq", split_axis=1, concat_axis=0, tiled=True),
        lax.all_to_all(steps_raw, "seq", split_axis=1, concat_axis=0, tiled=True),
        lax.all_to_all(queries, "seq", split_axis=1, concat_axis=0, tiled=True),
    )
    bcall, kvall = (
        lax.all_gather(bcpart, "seq", axis=0, tiled=True),
        lax.all_gather(keyvals, "seq", axis=0, tiled=True),
    )
    seq_index = lax.axis_index("seq")
    length = bcall.shape[0]
    heads = stepheads.shape[1]
    span = xheads.shape[1]
    kernel_x = lax.dynamic_slice_in_dim(kernel_all, seq_index * span, span, 0)
    bias_x = lax.dynamic_slice_in_dim(bias_all, seq_index * span, span, 0)
    mamba_args = (
        xheads.astype(jnp.float32),
        bcall.astype(jnp.float32),
        kernel_x.astype(jnp.float32),
        kernel_all[D_SSM:].astype(jnp.float32),
        bias_x.astype(jnp.float32),
        bias_all[D_SSM:].astype(jnp.float32),
        stepheads.astype(jnp.float32),
        lax.dynamic_slice_in_dim(step_bias, seq_index * heads, heads, 0),
        lax.dynamic_slice_in_dim(decay_log, seq_index * heads, heads, 0),
        lax.dynamic_slice_in_dim(skip_gain, seq_index * heads, heads, 0),
    )
    mamba_y, pullback = jax.vjp(mamba_heads, *mamba_args)
    cosine, sine = rope_tables(length, AP)
    key_rot = rotate(
        kvall[:, : KVH * AP].reshape(length, KVH, AP).astype(jnp.float32),
        cosine[:, None, :],
        sine[:, None, :],
    ).astype(jnp.bfloat16)
    value_heads = kvall[:, KVH * AP :].reshape(length, KVH, AP)
    local_heads = qheads.shape[1] // AP
    block = min(512, length)
    count = length // block
    positions = jnp.arange(length)
    starts = jnp.arange(count) * block
    scale = 1.0 / math.sqrt(AP)
    head = 0
    owner = (seq_index * local_heads + head) // (QH // KVH)
    key_head = lax.dynamic_index_in_dim(key_rot, owner, 1, keepdims=False)
    value_head = lax.dynamic_index_in_dim(value_heads, owner, 1, keepdims=False)
    query_rot = rotate(qheads.astype(jnp.float32), cosine, sine).astype(jnp.bfloat16)

    def forward_block(item):
        return attend(item[0], key_head, value_head, item[1] + jnp.arange(block), positions, scale)

    block_outs, block_lse = lax.map(forward_block, (query_rot.reshape(count, block, AP), starts))
    kept_heads = [(owner, key_head, value_head, query_rot, block_outs, block_lse)]
    head_outputs = block_outs.reshape(length, AP)
    mixed_y, attn_tok = (
        lax.all_to_all(
            mamba_y.astype(jnp.bfloat16), "seq", split_axis=0, concat_axis=1, tiled=True
        ),
        lax.all_to_all(head_outputs, "seq", split_axis=0, concat_axis=1, tiled=True),
    )
    block_out, saved = token_tail(
        resid,
        mixed_y,
        attn_tok,
        gate_pre,
        gain_gated,
        out_mixer,
        out_attn,
        gain_ffn,
        proj_gateup,
        proj_down,
    )
    backward_weights = (
        lax.all_gather(shards[0], "fsdp", axis=0, tiled=True),
        lax.all_gather(shards[1], "fsdp", axis=0, tiled=True),
        lax.all_gather(shards[2], "fsdp", axis=0, tiled=True),
        lax.all_gather(shards[3], "fsdp", axis=0, tiled=True),
        lax.all_gather(shards[4], "fsdp", axis=0, tiled=True),
        lax.all_gather(shards[5], "fsdp", axis=0, tiled=True),
        lax.all_gather(shards[6], "fsdp", axis=0, tiled=True),
        lax.all_gather(shards[7], "fsdp", axis=0, tiled=True),
        lax.all_gather(shards[8], "fsdp", axis=0, tiled=True),
        lax.all_gather(shards[9], "fsdp", axis=0, tiled=True),
        lax.all_gather(shards[10], "fsdp", axis=0, tiled=True),
    )
    (
        back_one,
        back_mixer,
        back_attn,
        back_kernel,
        back_bias,
        back_gated,
        back_mixout,
        back_attnout,
        back_ffn,
        back_gateup,
        back_down,
    ) = backward_weights

    def layout(value, axis):
        return value

    grad_middle, grad_ymix, grad_otok, grad_gate, late = token_back_tail(
        out_grad[0],
        saved,
        mixed_y,
        attn_tok,
        gate_pre,
        back_gated,
        back_mixout,
        back_attnout,
        back_ffn,
        back_gateup,
        back_down,
        layout,
    )
    ygrad_heads, ograd_heads = (
        lax.all_to_all(grad_ymix, "seq", split_axis=1, concat_axis=0, tiled=True),
        lax.all_to_all(grad_otok, "seq", split_axis=1, concat_axis=0, tiled=True),
    )
    xg, bcg, kxg, kbcg, bxg, bbcg, stepg, stepbg, decayg, skipg = pullback(
        ygrad_heads.astype(jnp.float32)
    )
    head = 0
    owner, key_head, value_head, query_rot, block_outs, block_lse = kept_heads[head]
    grad_head = ograd_heads.reshape(count, block, AP)

    def backward_block(carry, item):
        dquery, dkeys, dvals = attend_back(
            item[0],
            key_head,
            value_head,
            item[1],
            item[2],
            item[3],
            item[4] + jnp.arange(block),
            positions,
            scale,
        )
        return ((carry[0] + dkeys, carry[1] + dvals), dquery)

    empty = jnp.zeros((length, AP), jnp.float32)
    (key_grad, value_grad), query_blocks = lax.scan(
        backward_block,
        (empty, empty),
        (query_rot.reshape(count, block, AP), block_outs, block_lse, grad_head, starts),
    )
    query_grads = unrotate(query_blocks.reshape(length, AP), cosine, sine).astype(jnp.bfloat16)
    select = (jnp.arange(KVH) == owner).astype(jnp.float32)
    key_total = select[None, :, None] * unrotate(key_grad, cosine, sine)[:, None, :]
    value_total = select[None, :, None] * value_grad[:, None, :]
    kvgrad_all = jnp.concatenate(
        [key_total.reshape(length, KVH * AP), value_total.reshape(length, KVH * AP)], axis=1
    )
    xgrad, stepgrad, qgrad = (
        lax.all_to_all(xg.astype(jnp.bfloat16), "seq", split_axis=0, concat_axis=1, tiled=True),
        lax.all_to_all(stepg.astype(jnp.bfloat16), "seq", split_axis=0, concat_axis=1, tiled=True),
        lax.all_to_all(query_grads, "seq", split_axis=0, concat_axis=1, tiled=True),
    )
    bcgrad, kvgrad = (
        lax.psum_scatter(bcg.astype(jnp.bfloat16), "seq", scatter_dimension=0, tiled=True).astype(
            jnp.float32
        ),
        lax.psum_scatter(
            kvgrad_all.astype(jnp.bfloat16), "seq", scatter_dimension=0, tiled=True
        ).astype(jnp.float32),
    )
    input_grad, grad_norm, grad_mixer, grad_attn = token_back_front(
        grad_middle,
        grad_gate,
        xgrad,
        bcgrad,
        stepgrad,
        qgrad,
        kvgrad,
        normed_in,
        normed_one,
        scale_one,
        back_one,
        back_mixer,
        back_attn,
        layout,
    )
    kernel_grad = jnp.concatenate(
        [
            lax.dynamic_update_slice(
                jnp.zeros((D_SSM, kxg.shape[1]), jnp.float32), kxg, (seq_index * span, 0)
            ),
            kbcg,
        ],
        axis=0,
    )
    bias_grad = jnp.concatenate(
        [
            lax.dynamic_update_slice(jnp.zeros((D_SSM,), jnp.float32), bxg, (seq_index * span,)),
            bbcg,
        ],
        axis=0,
    )
    grad_gated, grad_mixed, grad_attended, grad_ffn, grad_gateup, grad_down = late
    grads = (
        layout(grad_norm, 0),
        grad_mixer,
        grad_attn,
        layout(kernel_grad, 0),
        layout(bias_grad, 0),
        layout(grad_gated, 0),
        grad_mixed,
        grad_attended,
        layout(grad_ffn, 0),
        grad_gateup,
        grad_down,
    )
    pieces = (
        lax.psum_scatter(
            grads[0].astype(jnp.bfloat16), "fsdp", scatter_dimension=0, tiled=True
        ).astype(jnp.float32),
        lax.psum_scatter(
            grads[1].astype(jnp.bfloat16), "fsdp", scatter_dimension=0, tiled=True
        ).astype(jnp.float32),
        lax.psum_scatter(
            grads[2].astype(jnp.bfloat16), "fsdp", scatter_dimension=0, tiled=True
        ).astype(jnp.float32),
        lax.psum_scatter(
            grads[3].astype(jnp.bfloat16), "fsdp", scatter_dimension=0, tiled=True
        ).astype(jnp.float32),
        lax.psum_scatter(
            grads[4].astype(jnp.bfloat16), "fsdp", scatter_dimension=0, tiled=True
        ).astype(jnp.float32),
        lax.psum_scatter(
            grads[5].astype(jnp.bfloat16), "fsdp", scatter_dimension=0, tiled=True
        ).astype(jnp.float32),
        lax.psum_scatter(
            grads[6].astype(jnp.bfloat16), "fsdp", scatter_dimension=0, tiled=True
        ).astype(jnp.float32),
        lax.psum_scatter(
            grads[7].astype(jnp.bfloat16), "fsdp", scatter_dimension=0, tiled=True
        ).astype(jnp.float32),
        lax.psum_scatter(
            grads[8].astype(jnp.bfloat16), "fsdp", scatter_dimension=0, tiled=True
        ).astype(jnp.float32),
        lax.psum_scatter(
            grads[9].astype(jnp.bfloat16), "fsdp", scatter_dimension=0, tiled=True
        ).astype(jnp.float32),
        lax.psum_scatter(
            grads[10].astype(jnp.bfloat16), "fsdp", scatter_dimension=0, tiled=True
        ).astype(jnp.float32),
    )
    summed = (
        lax.psum(pieces[0].astype(jnp.bfloat16), "seq").astype(jnp.float32),
        lax.psum(pieces[1].astype(jnp.bfloat16), "seq").astype(jnp.float32),
        lax.psum(pieces[2].astype(jnp.bfloat16), "seq").astype(jnp.float32),
        lax.psum(pieces[3].astype(jnp.bfloat16), "seq").astype(jnp.float32),
        lax.psum(pieces[4].astype(jnp.bfloat16), "seq").astype(jnp.float32),
        lax.psum(pieces[5].astype(jnp.bfloat16), "seq").astype(jnp.float32),
        lax.psum(pieces[6].astype(jnp.bfloat16), "seq").astype(jnp.float32),
        lax.psum(pieces[7].astype(jnp.bfloat16), "seq").astype(jnp.float32),
        lax.psum(pieces[8].astype(jnp.bfloat16), "seq").astype(jnp.float32),
        lax.psum(pieces[9].astype(jnp.bfloat16), "seq").astype(jnp.float32),
        lax.psum(pieces[10].astype(jnp.bfloat16), "seq").astype(jnp.float32),
    )
    step_full = lax.dynamic_update_slice(
        jnp.zeros((MH,), jnp.float32), stepbg, (seq_index * heads,)
    )
    decay_full = lax.dynamic_update_slice(
        jnp.zeros((MH,), jnp.float32), decayg, (seq_index * heads,)
    )
    skip_full = lax.dynamic_update_slice(jnp.zeros((MH,), jnp.float32), skipg, (seq_index * heads,))
    step_sum, decay_sum, skip_sum = lax.psum((step_full, decay_full, skip_full), ("seq", "fsdp"))
    return (
        block_out[None],
        input_grad[None],
        summed[0],
        summed[1],
        summed[2],
        summed[3],
        summed[4],
        step_sum,
        decay_sum,
        skip_sum,
        summed[5],
        summed[6],
        summed[7],
        summed[8],
        summed[9],
        summed[10],
    )


def solution(mesh):
    in_specs = (
        P("fsdp", "seq", None),
        P("fsdp"),
        P("fsdp", None),
        P("fsdp", None),
        P("fsdp", None),
        P("fsdp"),
        P(),
        P(),
        P(),
        P("fsdp"),
        P("fsdp", None),
        P("fsdp", None),
        P("fsdp"),
        P("fsdp", None),
        P("fsdp", None),
        P("fsdp", "seq", None),
    )
    out_specs = (
        P("fsdp", "seq", None),
        P("fsdp", "seq", None),
        P("fsdp"),
        P("fsdp", None),
        P("fsdp", None),
        P("fsdp", None),
        P("fsdp"),
        P(),
        P(),
        P(),
        P("fsdp"),
        P("fsdp", None),
        P("fsdp", None),
        P("fsdp"),
        P("fsdp", None),
        P("fsdp", None),
    )
    return jax.shard_map(
        per_device, mesh=mesh, in_specs=in_specs, out_specs=out_specs, check_vma=False
    )
```

profile of v0, /device:TPU:0, one launch (start us, length us, event | category | flops | bytes accessed | tf_op | source)
XLA Modules:
  0.0 1372.7 jit_solution(14992720068867842791)
XLA Ops:
  15.4 71.1 %all-reduce.32 = (bf16[1536]{0:T(1024)(128)(2,1)S(1)}, bf16[1024]{0:T(1024)(128)(2,1)S(1)}, bf16[1792]{0:T(1024)(128)(2,1)S(1)}, bf16[1024]{0:T(1024)(128)(2,1)S(1)}) all-reduce(bf16[1536]{0:T(1024)(128)(2,1)S(1)} %dynamic-update-slice.2, bf16[1024]{0:T(1024)(128)(2,1)S(1)} %dynamic-update-slice.1, ...), channel_id=1, replica_groups=mesh['seq'=8,'fsdp'=16] {'fsdp'}, use_global_device_ids=true, to_apply=%add.24 | all-reduce | flops 5376 | bytes 21504
  90.7 37.6 %all-gather.10.cloned.1.call-done = bf16[1024,3352]{1,0:T(8,128)(2,1)} async-done(((bf16[64,3352]{1,0:T(8,128)(2,1)}), bf16[1024,3352]{1,0:T(8,128)(2,1)}) %all-gather.10.cloned.1.call-update) | async-done | bytes 6864912 | tf_op jit(solution)/shard_map/all_gather | solution.py:338
  128.3 7.7 fusion.188
  142.3 19.7 %all-gather = bf16[16,112,4]{1,2,0:T(4,128)(2,1)S(1)} all-gather(bf16[1,112,4]{1,2,0:T(4,128)(2,1)S(1)} %bitcast.557), channel_id=1, replica_groups=mesh['seq'=8,'fsdp'=16] {'fsdp'}, dimensions={0}, use_global_device_ids=true | all-gather | bytes 15232 | tf_op jit(solution)/shard_map/all_gather | solution.py:340
  201.4 13.1 all-to-all-done
  234.0 17.6 %while.63 = (s32[]{:T(128)}, f32[3,64,128]{2,1,0:T(8,128)S(1)}, f32[8,3,64,128]{3,2,1,0:T(8,128)}, f32[8,3,1,1]{1,3,2,0:T(1,128)}, f32[8,3]{1,0:T(8,128)S(1)}, /...) while((s32[]{:T(128)}, f32[3,64,128]{2,1,0:T(8,128)S(1)}, f32[8,3,64,128]{3,2,1,0:T(8,128)}, ...), condition=%wide.region_4.5_spmd.clone, body=%wide.region_3.4_spmd.clone.sunk | while | flops 98307 | bytes 493208 | solution.py:95
  266.9 8.7 fusion.68
  279.1 38.1 %while.62 = (s32[]{:T(128)}, bf16[4,512,64]{1,2,0:T(8,128)(2,1)S(1)}, f32[4,512]{1,0:T(4,128)}, s32[4]{0:T(128)S(1)}, bf16[4,512,64]{2,1,0:T(8,128)(2,1)}, /*ind...) while((s32[]{:T(128)}, ...), condition=%wide.region_9.10_spmd.clone, body=%wide.region_6.9_spmd.clone.sunk | while | flops 277905408 | bytes 30368400 | solution.py:425
  318.3 5.8 all-to-all-start.4
  334.7 54.9 %all-gather.22.cloned.1.call-done = bf16[1024,4096]{1,0:T(8,128)(2,1)} async-done(((bf16[64,4096]{1,0:T(8,128)(2,1)}), bf16[1024,4096]{1,0:T(8,128)(2,1)}) %all-gather.22.cloned.1.call-update) | async-done | bytes 8388624 | tf_op jit(solution)/shard_map/all_gather | solution.py:346
  389.7 7.8 fusion.171
  397.4 47.9 %all-gather.24.cloned.1.call-done = bf16[2048,1024]{1,0:T(8,128)(2,1)} async-done(((bf16[128,1024]{1,0:T(8,128)(2,1)}), bf16[2048,1024]{1,0:T(8,128)(2,1)}) %all-gather.24.cloned.1.call-update) | async-done | bytes 4194320 | tf_op jit(solution)/shard_map/all_gather | solution.py:347
  445.3 6.5 multiply_convert_fusion.2
  480.9 87.3 %while.65 = (s32[]{:T(128)}, f32[2048,64]{0,1:T(8,128)}, f32[2048,64]{0,1:T(8,128)}, f32[4,512,64]{1,0,2:T(4,128)}, s32[4]{0:T(128)}, /*index=5*/bf16[4,512,64]{...) while((s32[]{:T(128)}, f32[2048,64]{0,1:T(8,128)}, ...), condition=%wide.region_27.28_spmd.clone, body=%wide.region_25.27_spmd.clone.sunk | while | flops 680296448 | bytes 29901136 | solution.py:516
  585.5 18.9 %while.64 = (s32[]{:T(128)}, f32[3,64,128]{2,1,0:T(8,128)S(1)}, f32[8,3]{1,0:T(8,128)S(1)}, f32[8,3,64,128]{3,2,1,0:T(8,128)}, f32[8,3,64,128]{3,2,1,0:T(8,128)}...) while((s32[]{:T(128)}, f32[3,64,128]{2,1,0:T(8,128)S(1)}, ...), condition=%wide.region_15.16_spmd.clone, body=%wide.region_13.15_spmd.clone.sunk | while | flops 147457 | bytes 590036 | solution.py:95
  604.5 8.4 fusion.39
  623.0 6.6 convolution_add_fusion.2
  632.2 7.3 multiply_reduce_fusion.3
  645.7 5.9 fusion.60
  664.8 15.3 %all_to_all.154 = bf16[8,256,64]{1,2,0:T(8,128)(2,1)S(1)} all-to-all(bf16[8,256,64]{1,2,0:T(8,128)(2,1)S(1)} %pad_maximum_fusion.10), channel_id=1, replica_groups=mesh['seq'=8,'fsdp'=16] {'seq'}, dimensions={0} | all-to-all | bytes 524288 | tf_op jit(solution)/shard_map/all_to_all | solution.py:531
  691.8 7.3 convolution_convert_fusion
  706.2 8.1 reduce-window.16
  729.2 10.2 all-to-all-done.6
  739.4 6.2 convolution_convert_fusion.1
  753.0 62.5 %all-reduce.30 = (f32[24]{0:T(128)}, f32[24]{0:T(128)}, f32[24]{0:T(128)}) all-reduce(f32[24]{0:T(128)S(1)} %dynamic_update_slice.56, f32[24]{0:T(128)S(1)} %multiply_dynamic-update-slice_fusion, f32[24]{0:T(128)S(1)} %dynamic_update_slice.58), channel_id=1, replica_groups=mesh['seq'=8,'fsdp'=16] {'seq','fsdp'}, use_global_device_ids=true, to_apply=%region_52.53 | all-reduce | flops 72 | bytes 576 | tf_op jit(solution)/shard_map/psum | solution.py:642
  821.4 72.4 %reduce-scatter.18.cloned.1.call-done = bf16[64,768]{1,0:T(8,128)(2,1)} async-done(((bf16[1024,768]{1,0:T(8,128)(2,1)}), bf16[64,768]{1,0:T(8,128)(2,1)}) %reduce-scatter.18.cloned.1.call-update) | async-done | bytes 98320 | tf_op jit(solution)/shard_map/reduce_scatter | solution.py:594
  893.9 78.4 %reduce-scatter.20.cloned.1.call-done = bf16[96,1024]{1,0:T(8,128)(2,1)} async-done(((bf16[1536,1024]{1,0:T(8,128)(2,1)}), bf16[96,1024]{1,0:T(8,128)(2,1)}) %reduce-scatter.20.cloned.1.call-update) | async-done | bytes 196624 | tf_op jit(solution)/shard_map/reduce_scatter | solution.py:606
  972.3 83.3 %reduce-scatter.26.cloned.1.call-done = bf16[128,1024]{1,0:T(8,128)(2,1)} async-done(((bf16[2048,1024]{1,0:T(8,128)(2,1)}), bf16[128,1024]{1,0:T(8,128)(2,1)}) %reduce-scatter.26.cloned.1.call-update) | async-done | bytes 262160 | tf_op jit(solution)/shard_map/reduce_scatter | solution.py:618
  1055.6 106.0 %reduce-scatter.24.cloned.1.call-done = bf16[64,4096]{1,0:T(8,128)(2,1)} async-done(((bf16[1024,4096]{1,0:T(8,128)(2,1)}), bf16[64,4096]{1,0:T(8,128)(2,1)}) %reduce-scatter.24.cloned.1.call-update) | async-done | bytes 524304 | tf_op jit(solution)/shard_map/reduce_scatter | solution.py:615
  1161.6 96.7 %reduce-scatter.16.cloned.1.call-done = bf16[64,3352]{1,0:T(8,128)(2,1)} async-done(((bf16[1024,3352]{1,0:T(8,128)(2,1)}), bf16[64,3352]{1,0:T(8,128)(2,1)}) %reduce-scatter.16.cloned.1.call-update) | async-done | bytes 429072 | tf_op jit(solution)/shard_map/reduce_scatter | solution.py:591
  1265.9 65.4 %all-reduce.31 = (bf16[1024]{0:T(1024)(128)(2,1)S(1)}, bf16[1792]{0:T(1024)(128)(2,1)S(1)}, bf16[1536]{0:T(1024)(128)(2,1)S(1)}, bf16[1024]{0:T(1024)(128)(2,1)S(1)}) all-reduce(bf16[1024]{0:T(1024)(128)(2,1)S(1)} %get-tuple-element.608, ...), channel_id=4, replica_groups=mesh['seq'=8,'fsdp'=16] {'fsdp'}, use_global_device_ids=true, to_apply=%region_31.32.clone | all-reduce | flops 5376 | bytes 21504
  1331.6 21.5 %all-reduce.33 = (bf16[64]{0:T(256)(128)(2,1)S(1)}, bf16[112,4]{0,1:T(4,128)(2,1)S(1)}, bf16[112]{0:T(256)(128)(2,1)S(1)}, bf16[96]{0:T(256)(128)(2,1)S(1)}, bf16[64]{0:T(256)(128)(2,1)S(1)}) all-reduce(bf16[64]{0:T(256)(128)(2,1)S(1)} %dynamic-slice.5, bf16[112,4]{0,1:T(4,128)(2,1)S(1)} %copy.522, ...), channel_id=1, replica_groups=mesh['seq'=8,'fsdp'=16] {'seq'}, use_global_device_ids=true, to_apply=%region_32.33 | all-reduce | flops 784 | bytes 3136 | tf_op jit(solution)/shard_map/psum | solution.py:623
  (680 shorter events, 409.2 us)
Async XLA Ops:
  7.2 80.5 %all-gather.16.cloned.1.call-start = ((), (), s32[]{:S(2)}) async-start(), calls=%async_computation.22 | async-start | bytes 1671168 | tf_op jit(solution)/shard_map/all_gather | solution.py:339
  7.9 120.3 %all-gather.10.cloned.1.call-start = ((), (), s32[]{:S(2)}) async-start(), calls=%async_computation.19 | async-start | bytes 7520256 | tf_op jit(solution)/shard_map/all_gather | solution.py:338
  8.7 119.6 %copy-start.17 = (bf16[1,256,1024]{2,1,0:T(8,128)(2,1)S(1)}, bf16[1,256,1024]{2,1,0:T(8,128)(2,1)}, u32[]{:S(2)}) copy-start(bf16[1,256,1024]{2,1,0:T(8,128)(2,1)} %param.24) | copy-start | bytes 1572868
  8.7 171.7 %all-gather.18.cloned.1.call-start = ((), (), s32[]{:S(2)}) async-start(), calls=%async_computation.23 | async-start | bytes 1179648 | tf_op jit(solution)/shard_map/all_gather | solution.py:382
  90.6 128.2 %all-gather.12.cloned.1.call-start = ((), (), s32[]{:S(2)}) async-start(), calls=%async_computation.20 | async-start | bytes 1179648 | tf_op jit(solution)/shard_map/all_gather | solution.py:381
  137.9 190.3 %all-gather.14.cloned.1.call-start = ((), (), s32[]{:S(2)}) async-start(), calls=%async_computation.21 | async-start | bytes 3342336 | tf_op jit(solution)/shard_map/all_gather | solution.py:343
  138.5 193.9 %all-gather.20.cloned.1.call-start = ((), (), s32[]{:S(2)}) async-start(), calls=%async_computation.24 | async-start | bytes 1114112 | tf_op jit(solution)/shard_map/all_gather | solution.py:344
  139.1 250.6 %all-gather.22.cloned.1.call-start = ((), (), s32[]{:S(2)}) async-start(), calls=%async_computation.25 | async-start | bytes 8912896 | tf_op jit(solution)/shard_map/all_gather | solution.py:346
  139.8 305.5 %all-gather.24.cloned.1.call-start = ((), (), s32[]{:S(2)}) async-start(), calls=%async_computation.26 | async-start | bytes 4456448 | tf_op jit(solution)/shard_map/all_gather | solution.py:347
  163.8 13.0 all-to-all-start.3
  184.7 9.5 all-to-all-start.1
  194.2 20.3 %all-to-all-start = ((bf16[256,8,192]{0,2,1:T(8,128)(2,1)}), bf16[256,8,192]{0,2,1:T(8,128)(2,1)S(1)}, u32[]{:S(2)}, u32[]{:S(2)}) async-start(bf16[256,8,192]{0,2,1:T(8,128)(2,1)} %bitcast.6), calls=%async_computation | async-start | bytes 1572864 | tf_op jit(solution)/shard_map/all_to_all | solution.py:376
  275.5 42.8 %all-to-all-start.2 = ((bf16[8,256,192]{1,2,0:T(8,128)(2,1)}), bf16[8,256,192]{1,2,0:T(8,128)(2,1)S(1)}, u32[]{:S(2)}, u32[]{:S(2)}) async-start(bf16[8,256,192]{1,2,0:T(8,128)(2,1)} %bitcast.517), calls=%async_computation.2 | async-start | bytes 1572864 | tf_op jit(solution)/shard_map/all_to_all | solution.py:429
  318.3 14.1 %all-to-all-start.4 = ((bf16[8,256,64]{1,2,0:T(8,128)(2,1)}), bf16[8,256,64]{1,2,0:T(8,128)(2,1)S(1)}, u32[]{:S(2)}, u32[]{:S(2)}) async-start(bf16[8,256,64]{1,2,0:T(8,128)(2,1)} %copy.457), calls=%async_computation.4 | async-start | bytes 524288 | tf_op jit(solution)/shard_map/all_to_all | solution.py:432
  463.9 12.4 all-to-all-start.8
  476.3 98.4 %all-to-all-start.5 = ((bf16[256,8,192]{0,2,1:T(8,128)(2,1)}), bf16[256,8,192]{0,2,1:T(8,128)(2,1)}, u32[]{:S(2)}, u32[]{:S(2)}) async-start(bf16[256,8,192]{0,2,1:T(8,128)(2,1)} %bitcast.39), calls=%async_computation.5 | async-start | bytes 1572864 | tf_op jit(solution)/shard_map/all_to_all | solution.py:491
  480.6 199.5 %reduce-scatter.14.cloned.1.call-start = ((), (), s32[]{:S(2)}) async-start(), calls=%async_computation.28 | async-start | bytes 1179648 | tf_op jit(solution)/shard_map/reduce_scatter | solution.py:537
  574.7 164.7 %reduce-scatter.12.cloned.1.call-start = ((), (), s32[]{:S(2)}) async-start(), calls=%async_computation.27 | async-start | bytes 1179648 | tf_op jit(solution)/shard_map/reduce_scatter | solution.py:534
  642.8 173.0 %reduce-scatter.28.cloned.1.call-start = ((), (), s32[]{:S(2)}) async-start(), calls=%async_computation.35 | async-start | bytes 487424
  661.2 160.3 %reduce-scatter.22.cloned.1.call-start = ((), (), s32[]{:S(2)}) async-start(), calls=%async_computation.32 | async-start | bytes 1114112 | tf_op jit(solution)/shard_map/reduce_scatter | solution.py:609
  663.8 230.1 %reduce-scatter.18.cloned.1.call-start = ((), (), s32[]{:S(2)}) async-start(), calls=%async_computation.30 | async-start | bytes 1671168 | tf_op jit(solution)/shard_map/reduce_scatter | solution.py:594
  682.8 289.4 %reduce-scatter.20.cloned.1.call-start = ((), (), s32[]{:S(2)}) async-start(), calls=%async_computation.31 | async-start | bytes 3342336 | tf_op jit(solution)/shard_map/reduce_scatter | solution.py:606
  686.8 368.8 %reduce-scatter.26.cloned.1.call-start = ((), (), s32[]{:S(2)}) async-start(), calls=%async_computation.34 | async-start | bytes 4456448 | tf_op jit(solution)/shard_map/reduce_scatter | solution.py:618
  691.8 469.9 %reduce-scatter.24.cloned.1.call-start = ((), (), s32[]{:S(2)}) async-start(), calls=%async_computation.33 | async-start | bytes 8912896 | tf_op jit(solution)/shard_map/reduce_scatter | solution.py:615
  716.1 9.5 all-to-all-start.7
  725.6 13.8 %all-to-all-start.6 = ((bf16[8,256,192]{1,2,0:T(8,128)(2,1)}), bf16[8,256,192]{1,2,0:T(8,128)(2,1)S(1)}, u32[]{:S(2)}, u32[]{:S(2)}) async-start(bf16[8,256,192]{1,2,0:T(8,128)(2,1)} %bitcast.425), calls=%async_computation.6 | async-start | bytes 1572864 | tf_op jit(solution)/shard_map/all_to_all | solution.py:529
  729.1 529.2 %reduce-scatter.16.cloned.1.call-start = ((), (), s32[]{:S(2)}) async-start(), calls=%async_computation.29 | async-start | bytes 7520256 | tf_op jit(solution)/shard_map/reduce_scatter | solution.py:591
  745.6 612.9 %all-reduce.37.cloned.1.call-start = ((), (), s32[]{:S(2)}) async-start(), calls=%async_computation.36 | async-start | bytes 3178496 | tf_op jit(solution)/shard_map/psum | solution.py:624
  748.7 509.6 %copy-start.112 = (bf16[256,256]{0,1:T(8,128)(2,1)S(1)}, bf16[256,256]{0,1:T(8,128)(2,1)}, u32[]{:S(2)}) copy-start(bf16[256,256]{0,1:T(8,128)(2,1)} %reduce-scatter.12.cloned.1.call-done) | copy-start | bytes 393220
  1264.2 91.6 %copy-start.30 = (bf16[1,256,1024]{2,1,0:T(8,128)(2,1)S(1)}, bf16[1,256,1024]{2,1,0:T(8,128)(2,1)}, u32[]{:S(2)}) copy-start(bf16[1,256,1024]{2,1,0:T(8,128)(2,1)} %param.39) | copy-start | bytes 1572868
  1264.2 91.6 %copy-start.34 = (f32[256,1024]{1,0:T(8,128)S(1)}, f32[256,1024]{1,0:T(8,128)}, u32[]{:S(2)}) copy-start(f32[256,1024]{1,0:T(8,128)} %copy-done.33) | copy-start | bytes 3145732
  1264.2 91.6 %copy-start.77 = (f32[256]{0:T(256)S(1)}, f32[256]{0:T(256)}, u32[]{:S(2)}) copy-start(f32[256]{0:T(256)} %copy-done.76) | copy-start | bytes 3076
  (134 other events, 1845.7 us)
Sparse Core Ops, SparseCore 0:
  10.5 48.9 all-gather.15
  61.9 66.2 all-gather.9
  130.5 37.9 all-gather.17
  170.5 44.2 all-gather.11
  217.1 52.1 all-gather.13
  271.6 43.6 all-gather.19
  317.8 71.8 all-gather.21
  392.1 53.1 all-gather.23
  574.8 40.2 reduce-scatter.13
  642.9 40.8 reduce-scatter.11
  688.1 62.9 reduce-scatter.27
  755.3 66.0 reduce-scatter.21
  825.9 67.9 reduce-scatter.17
  897.8 74.4 reduce-scatter.19
  976.1 79.4 reduce-scatter.25
  1060.3 101.2 reduce-scatter.23
  1166.3 91.9 reduce-scatter.15
  1261.2 90.8 all-reduce.36
where the time goes:
time: 1380 us; the launch traced here: 1370 us
  waiting for transfers between devices  625 us (45%)
  blocking collectives  255 us (18%)
  matrix products  217 us (16%)
  other arithmetic  115 us (8%)
  local copies, waits for them, and re-layouts  101 us (7%)
  starting transfers between devices  38.8 us (3%)
  between operations  20.2 us (1%)
    unnamed x2, blocking collectives  136 us
    reduce_scatter x1, waiting for transfers between devices, per_device(): lax.psum_scatter(grads[9].astype(jnp.bfloat16), 'fsdp', scatter_dimension...  106 us
    reduce_scatter x1, waiting for transfers between devices, per_device(): lax.psum_scatter(grads[1].astype(jnp.bfloat16), 'fsdp', scatter_dimension...  96.7 us
    reduce_scatter x1, waiting for transfers between devices, per_device(): lax.psum_scatter(grads[10].astype(jnp.bfloat16), 'fsdp', scatter_dimensio...  83.3 us
    reduce_scatter x1, waiting for transfers between devices, per_device(): lax.psum_scatter(grads[6].astype(jnp.bfloat16), 'fsdp', scatter_dimension...  78.4 us
    reduce_scatter x1, waiting for transfers between devices, per_device(): lax.psum_scatter(grads[2].astype(jnp.bfloat16), 'fsdp', scatter_dimension...  72.4 us
    psum x1, blocking collectives, per_device(): lax.psum((step_full, decay_full, skip_full), ('seq', 'fsdp'))  62.5 us
    all_gather x1, waiting for transfers between devices, per_device(): lax.all_gather(shards[9], 'fsdp', axis=0, tiled=True)  54.9 us
  transfers between devices with their start and end apart: 27, of which 15 were waited for; matrix products, arithmetic and copies ran while one was open for 29% of the time, Pallas kernels for 0%

commit v1 on v0

v1 whole, which is shorter than its diff:
```python
import functools
import math

import jax
import jax.numpy as jnp
from jax import lax
from jax.experimental import pallas as pl
from jax.experimental.pallas import tpu as pltpu
from jax.sharding import PartitionSpec as P

MH = 24
NST = 128
QH = 8
KVH = 2
AP = 64
FF = 2048
D_SSM = 1536
XBC = 1792
CIN = 3352
FRONT = 4224
EPSILON = 1e-05
THETA = 10000.0
HIGHEST = lax.Precision.HIGHEST
F32 = jnp.float32
BF = jnp.bfloat16
NT = (((1,), (1,)), ((), ()))
TN = (((0,), (0,)), ((), ()))


def dot(a, b, dims=(((1,), (0,)), ((), ())), precision=None):
    return lax.dot_general(a, b, dims, preferred_element_type=F32, precision=precision)


def silu_slope(value):
    sigma = jax.nn.sigmoid(value)
    return sigma * (1.0 + value * (1.0 - sigma))


def rms_scale(value):
    return lax.rsqrt(jnp.mean(value * value, axis=1, keepdims=True) + EPSILON)


def rms_back(grad_normed, normed, scale):
    return scale * (grad_normed - normed * jnp.mean(grad_normed * normed, axis=1, keepdims=True))


def head_selector(rows, cols):
    channel = lax.broadcasted_iota(jnp.int32, (rows, cols), 0)
    head = lax.broadcasted_iota(jnp.int32, (rows, cols), 1)
    return jnp.where((channel >= head * AP) & (channel < head * AP + AP), 1.0, 0.0).astype(F32)


def spread_heads(value):
    head = lax.broadcasted_iota(jnp.int32, (128, D_SSM), 0)
    channel = lax.broadcasted_iota(jnp.int32, (128, D_SSM), 1)
    select = jnp.where((channel >= head * AP) & (channel < head * AP + AP), 1.0, 0.0).astype(F32)
    return dot(value, select, precision=HIGHEST)


def gather_heads(value):
    return dot(value, head_selector(D_SSM, 128), precision=HIGHEST)


def conv_pre(ext, taps, bias, length):
    result = bias[...] + taps[3:4, :] * ext[8 : 8 + length, :]
    for lag in range(3):
        result = result + taps[lag : lag + 1, :] * ext[pl.ds(5 + lag, length), :]
    return result


def mamba_first(xbc, halo, steps, taps, bias, sbias, dlog, act_ref, dt_ref, cum_ref, fresh_ref, ext):
    length = xbc.shape[0]
    ext[0:8, :] = halo[...].astype(F32)
    ext[8 : 8 + length, :] = xbc[...].astype(F32)
    conv = conv_pre(ext, taps, bias, length)
    act = conv * jax.nn.sigmoid(conv)
    act_ref[...] = act
    lane = lax.broadcasted_iota(jnp.int32, (length, 128), 1)
    raw = steps[...].astype(F32) + sbias[...]
    dt = jnp.maximum(raw, 0.0) + jnp.log1p(jnp.exp(-jnp.abs(raw)))
    dt = jnp.where(lane < MH, dt, 0.0)
    dt_ref[...] = dt
    row = lax.broadcasted_iota(jnp.int32, (length, length), 0)
    col = lax.broadcasted_iota(jnp.int32, (length, length), 1)
    lower = jnp.where(row >= col, 1.0, 0.0).astype(F32)
    cum = dot(lower, dt * (-jnp.exp(dlog[...])), precision=HIGHEST)
    cum_ref[...] = cum
    weight = spread_heads(jnp.exp(cum[length - 1 : length, :] - cum) * dt)
    scaled = (act[:, :D_SSM] * weight).astype(BF)
    fresh_ref[...] = dot(scaled, act[:, D_SSM : D_SSM + NST].astype(BF), TN).astype(BF)


def mamba_second(act, dt, cum, starts, skip, y_ref):
    length = act.shape[0]
    cumv = cum[...]
    cum_t = cumv.T
    bmat = act[:, D_SSM : D_SSM + NST].astype(BF)
    cmat = act[:, D_SSM + NST :].astype(BF)
    inner = dot(cmat, bmat, NT)
    row = lax.broadcasted_iota(jnp.int32, (length, length), 0)
    col = lax.broadcasted_iota(jnp.int32, (length, length), 1)
    inner = jnp.where(row >= col, inner, 0.0)
    x = act[:, :D_SSM]
    scaled = (x * spread_heads(dt[...])).astype(BF)
    outer = dot(cmat, starts[...], NT) * spread_heads(jnp.exp(cumv))
    base = outer + spread_heads(skip[...]) * x
    for pair in range(MH // 2):
        parts = []
        for h in (2 * pair, 2 * pair + 1):
            fade = jnp.exp(jnp.minimum(cumv[:, h : h + 1] - cum_t[h : h + 1, :], 0.0))
            parts.append(dot((inner * fade).astype(BF), scaled[:, h * AP : h * AP + AP]))
        lanes = slice(pair * 128, pair * 128 + 128)
        y_ref[:, lanes] = (base[:, lanes] + jnp.concatenate(parts, axis=1)).astype(BF)


def mamba_back_first(gy, act, cum, dstart_ref):
    rise = spread_heads(jnp.exp(cum[...]))
    cmat = act[:, D_SSM + NST :].astype(BF)
    dstart_ref[...] = dot((gy[...].astype(F32) * rise).astype(BF), cmat, TN).astype(BF)


def mamba_back_second(
    gy, xbc, halo, act, dt, cum, starts, dends, steps, taps, bias, sbias, dlog, skip,
    dconv_ref, dtaps_ref, dbias_ref, dsteps_ref, dhead_ref, ext, dact,
):
    length = act.shape[0]
    cumv = cum[...]
    dtv = dt[...]
    cum_t = cumv.T
    lane = lax.broadcasted_iota(jnp.int32, (length, 128), 1)
    bmat = act[:, D_SSM : D_SSM + NST].astype(BF)
    cmat = act[:, D_SSM + NST :].astype(BF)
    row = lax.broadcasted_iota(jnp.int32, (length, length), 0)
    col = lax.broadcasted_iota(jnp.int32, (length, length), 1)
    inner_t = jnp.where(col >= row, dot(bmat, cmat, NT), 0.0)
    x = act[:, :D_SSM]
    gyb = gy[...]
    gyf = gyb.astype(F32)
    dt_full = spread_heads(dtv)
    tail = spread_heads(jnp.exp(cumv[length - 1 : length, :] - cumv))
    rise = spread_heads(jnp.exp(cumv))
    xs = x * dt_full
    xsb = xs.astype(BF)
    ginner = jnp.zeros((length, length), F32)
    qcols = jnp.zeros((length, 128), F32)
    rrows = []
    for pair in range(MH // 2):
        parts = []
        for h in (2 * pair, 2 * pair + 1):
            lanes = slice(h * AP, h * AP + AP)
            fade = jnp.exp(jnp.minimum(cum_t[h : h + 1, :] - cumv[:, h : h + 1], 0.0))
            graded = dot(xsb[:, lanes], gyb[:, lanes], NT) * fade
            ginner = ginner + graded
            weighed = graded * inner_t
            rrows.append(jnp.sum(weighed, axis=0, keepdims=True))
            qcols = jnp.where(lane == h, jnp.sum(weighed, axis=1, keepdims=True), qcols)
            parts.append(dot((inner_t * fade).astype(BF), gyb[:, lanes]))
        dact[:, pair * 128 : pair * 128 + 128] = jnp.concatenate(parts, axis=1)
    ginner = jnp.where(col >= row, ginner, 0.0).astype(BF)
    rrows = jnp.concatenate(rrows + [jnp.zeros((128 - MH, length), F32)], axis=0).T
    endb = dends[...]
    startb = starts[...]
    from_end = dot(bmat, endb, NT) * tail
    dxs = dact[:, :D_SSM] + from_end
    reach = gather_heads(xs * from_end)
    outer = dot(cmat, startb, NT) * rise
    dcum = rrows - qcols + gather_heads(gyf * outer) - reach
    total = jnp.exp(cumv[length - 1 : length, :])
    carried = gather_heads_rows(startb, endb) * total + jnp.sum(reach, axis=0, keepdims=True)
    last = lax.broadcasted_iota(jnp.int32, (length, 128), 0) == length - 1
    dcum = dcum + jnp.where(last, carried, 0.0)
    upper = jnp.where(col >= row, 1.0, 0.0).astype(F32)
    rest = dot(upper, dcum, precision=HIGHEST)
    decay = -jnp.exp(dlog[...])
    ddt = gather_heads(x * dxs) + decay * rest
    ddecay = jnp.sum(dtv * rest, axis=0, keepdims=True) * decay
    raw = steps[...].astype(F32) + sbias[...]
    dsteps = jnp.where(lane < MH, ddt * jax.nn.sigmoid(raw), 0.0)
    dsteps_ref[...] = dsteps.astype(BF)
    dskip = gather_heads(jnp.sum(x * gyf, axis=0, keepdims=True))
    dhead_ref[0:1, :] = jnp.sum(dsteps, axis=0, keepdims=True)
    dhead_ref[1:2, :] = ddecay
    dhead_ref[2:3, :] = dskip
    dhead_ref[3:8, :] = jnp.zeros((5, 128), F32)
    dact[:, :D_SSM] = dt_full * dxs + spread_heads(skip[...]) * gyf
    dact[:, D_SSM : D_SSM + NST] = dot((xs * tail).astype(BF), endb) + dot(ginner, cmat)
    dact[:, D_SSM + NST :] = dot((gyf * rise).astype(BF), startb) + dot(ginner, bmat, TN)
    ext[0:8, :] = halo[...].astype(F32)
    ext[8 : 8 + length, :] = xbc[...].astype(F32)
    conv = conv_pre(ext, taps, bias, length)
    dconv = dact[...] * silu_slope(conv)
    dconv_ref[...] = dconv
    dbias_ref[...] = jnp.broadcast_to(jnp.sum(dconv, axis=0, keepdims=True), (8, XBC))
    for lag in range(4):
        dtaps_ref[lag : lag + 1, :] = jnp.sum(
            dconv * ext[pl.ds(5 + lag, length), :], axis=0, keepdims=True
        )
    dtaps_ref[4:8, :] = jnp.zeros((4, XBC), F32)


def gather_heads_rows(a, b):
    product = a.astype(F32) * b.astype(F32)
    per_row = dot(jnp.ones((8, NST), F32), product, NT, precision=HIGHEST)
    return gather_heads(per_row)[0:1, :]


def attend_forward(axis, q, kv, o_ref, lse_ref, acc, top, total):
    me = lax.axis_index(axis)
    block = q.shape[0]
    scale = 1.0 / math.sqrt(AP)
    acc[...] = jnp.zeros_like(acc)
    top[...] = jnp.full(top.shape, -jnp.inf, F32)
    total[...] = jnp.zeros_like(total)
    key_at = lax.broadcasted_iota(jnp.int32, (block, block), 0)
    query_at = lax.broadcasted_iota(jnp.int32, (block, block), 1)

    def step(j, carry):
        rows = pl.ds(pl.multiple_of(j * block, block), block)
        allowed = (key_at + j * block) <= (query_at + me * block)
        for h in range(QH):
            g = h // (QH // KVH)
            keys = kv[rows, g * AP : g * AP + AP]
            values = kv[rows, KVH * AP + g * AP : KVH * AP + g * AP + AP]
            s = dot(keys, q[:, h * AP : h * AP + AP], NT) * scale
            s = jnp.where(allowed, s, -1e30)
            old = top[h : h + 1, :]
            new = jnp.maximum(old, jnp.max(s, axis=0, keepdims=True))
            p = jnp.exp(s - new)
            fix = jnp.exp(old - new)
            top[h : h + 1, :] = new
            total[h : h + 1, :] = total[h : h + 1, :] * fix + jnp.sum(p, axis=0, keepdims=True)
            band = slice(h * AP, h * AP + AP)
            acc[band, :] = acc[band, :] * fix + dot(values, p.astype(BF), TN)
        return carry

    lax.fori_loop(0, me + 1, step, 0)
    lse_ref[...] = top[...] + jnp.log(total[...])
    for pair in range(QH // 2):
        parts = []
        for h in (2 * pair, 2 * pair + 1):
            parts.append(acc[h * AP : h * AP + AP, :] / total[h : h + 1, :])
        o_ref[:, pair * 128 : pair * 128 + 128] = jnp.concatenate(parts, axis=0).T.astype(BF)


def attend_backward(axis, q, kv, o, lse, go, dq_ref, dkv_ref):
    me = lax.axis_index(axis)
    block = q.shape[0]
    scale = 1.0 / math.sqrt(AP)
    dq_ref[...] = jnp.zeros_like(dq_ref)
    dkv_ref[...] = jnp.zeros_like(dkv_ref)
    key_at = lax.broadcasted_iota(jnp.int32, (block, block), 0)
    query_at = lax.broadcasted_iota(jnp.int32, (block, block), 1)
    centred = go[...].astype(F32) * o[...].astype(F32)
    pick_h = lax.broadcasted_iota(jnp.int32, (8, QH * AP), 0)
    pick_c = lax.broadcasted_iota(jnp.int32, (8, QH * AP), 1)
    pick = jnp.where((pick_c >= pick_h * AP) & (pick_c < pick_h * AP + AP), 1.0, 0.0).astype(F32)
    centre = dot(pick, centred, NT, precision=HIGHEST)

    def step(j, carry):
        rows = pl.ds(pl.multiple_of(j * block, block), block)
        allowed = (key_at + j * block) <= (query_at + me * block)
        sums = []
        for g in range(KVH):
            keys = kv[rows, g * AP : g * AP + AP]
            values = kv[rows, KVH * AP + g * AP : KVH * AP + g * AP + AP]
            dk = jnp.zeros((block, AP), F32)
            dv = jnp.zeros((block, AP), F32)
            for h in range(g * (QH // KVH), (g + 1) * (QH // KVH)):
                band = slice(h * AP, h * AP + AP)
                qh = q[:, band]
                gh = go[:, band]
                s = dot(keys, qh, NT) * scale
                p = jnp.exp(jnp.where(allowed, s - lse[h : h + 1, :], -1e30))
                dv = dv + dot(p.astype(BF), gh)
                dp = dot(values, gh, NT)
                ds = (p * (dp - centre[h : h + 1, :])).astype(BF)
                dk = dk + dot(ds, qh)
                dq_ref[:, band] += dot(ds, keys, TN) * scale
            sums.append((dk * scale, dv))
        dkv_ref[rows, 0:128] = jnp.concatenate([sums[0][0], sums[1][0]], axis=1).astype(BF)
        dkv_ref[rows, 128:256] = jnp.concatenate([sums[0][1], sums[1][1]], axis=1).astype(BF)
        return carry

    lax.fori_loop(0, me + 1, step, 0)


def call(kernel, outs, *args, scratch=(), limit=48):
    spec = pl.BlockSpec(memory_space=pltpu.VMEM)
    return pl.pallas_call(
        kernel,
        out_shape=[jax.ShapeDtypeStruct(shape, dtype) for shape, dtype in outs],
        in_specs=[spec] * len(args),
        out_specs=[spec] * len(outs),
        scratch_shapes=list(scratch),
        compiler_params=pltpu.CompilerParams(vmem_limit_bytes=limit << 20),
    )(*args)


def rope_parts(length, start):
    half = AP // 2
    inverse = THETA ** (-2.0 * jnp.arange(half).astype(F32) / AP)
    angles = (start + jnp.arange(length)).astype(F32)[:, None] * inverse[None, :]
    cosine = jnp.cos(angles)
    sine = jnp.sin(angles)
    return jnp.concatenate([cosine, cosine], axis=1), jnp.concatenate([-sine, sine], axis=1)


def swap_halves(value):
    rows, cols = value.shape
    parts = value.reshape(rows, cols // AP, 2, AP // 2)
    return parts[:, :, ::-1, :].reshape(rows, cols)


def pad_lanes(value):
    return jnp.pad(value.astype(F32), (0, 128 - value.shape[0]))[None, :]


def state_scan(packed, seqs):
    states = packed[:, :, :AP, :].astype(F32)
    logs = packed[:, :, AP, 0].astype(F32) + packed[:, :, AP + 1, 0].astype(F32)
    return states, jnp.exp(logs)


def per_device(
    seqs, hidden_in, norm_gain, mixer_proj, attn_proj, conv_kernel, conv_bias, step_bias, decay_log,
    skip_gain, gated_gain, mixer_out, attn_out, ffn_gain, gate_up, down_proj, out_grad,
):
    T = hidden_in.shape[1]
    width = norm_gain.shape[0]
    shards = 1024 // width
    me = lax.axis_index("seq")
    mix_rows, att_rows, down_rows = mixer_out.shape[0], attn_out.shape[0], down_proj.shape[0]

    small = jnp.concatenate(
        [norm_gain, ffn_gain, gated_gain, conv_bias, conv_kernel.T.reshape(-1)]
    )
    slots = width * 104
    small = jnp.pad(small, (0, slots - small.shape[0])).reshape(width, 104)
    front_shard = jnp.concatenate(
        [mixer_proj[:, : D_SSM + XBC], attn_proj, mixer_proj[:, D_SSM + XBC :], small], axis=1
    )
    front = lax.all_gather(front_shard, "fsdp", axis=0, tiled=True)
    tail_shard = jnp.concatenate(
        [
            gate_up[:, :FF],
            gate_up[:, FF:],
            jnp.concatenate([jnp.concatenate([mixer_out, attn_out], axis=0), down_proj], axis=1),
        ],
        axis=0,
    )
    tail_shard, _ = lax.optimization_barrier((tail_shard, front_shard))
    tail = lax.all_gather(tail_shard, "fsdp", axis=0, tiled=False)
    smalls = front.reshape(shards, width, FRONT)[:, :, 4120:].reshape(shards, slots)
    cuts = []
    at = 0
    for size in (width, width, gated_gain.shape[0], conv_bias.shape[0]):
        cuts.append(smalls[:, at : at + size].reshape(1, -1).astype(F32))
        at += size
    gain_one, gain_ffn, gain_gated, bias_all = cuts
    kernel_size = conv_kernel.shape[0]
    taps = smalls[:, at : at + 4 * kernel_size].reshape(shards, 4, kernel_size)
    taps = taps.transpose(1, 0, 2).reshape(4, XBC).astype(F32)
    taps = jnp.pad(taps, ((0, 4), (0, 0)))

    resid = hidden_in[0].astype(F32)
    scale_one = rms_scale(resid)
    normed_one = resid * scale_one
    normed_in = (normed_one * gain_one).astype(BF)
    projection = dot(normed_in, front)
    gate_pre = projection[:, :D_SSM]
    xbc = projection[:, D_SSM : D_SSM + XBC].astype(BF)
    queries = projection[:, 3328:3840].astype(BF)
    keyvals = projection[:, 3840:4096].astype(BF)
    steps = projection[:, 4096:].astype(BF)
    cosine, sine = rope_parts(T, me * T)
    cos_q, sin_q = jnp.tile(cosine, (1, QH)), jnp.tile(sine, (1, QH))
    cos_k, sin_k = jnp.tile(cosine, (1, KVH)), jnp.tile(sine, (1, KVH))
    query_rot = queries.astype(F32)
    query_rot = (query_rot * cos_q + swap_halves(query_rot) * sin_q).astype(BF)
    keys = keyvals[:, : KVH * AP].astype(F32)
    key_rot = (keys * cos_k + swap_halves(keys) * sin_k).astype(BF)
    kv_own = jnp.concatenate([key_rot, keyvals[:, KVH * AP :]], axis=1)
    halo = lax.ppermute(xbc[-8:], "seq", [(i, i + 1) for i in range(seqs - 1)])
    kv_all = lax.all_gather(kv_own, "seq", axis=0, tiled=True)
    sbias, dlog, skip = pad_lanes(step_bias), pad_lanes(decay_log), pad_lanes(skip_gain)
    act, dt, cum, fresh = call(
        mamba_first,
        [((T, XBC), F32), ((T, 128), F32), ((T, 128), F32), ((D_SSM, NST), BF)],
        xbc, halo, steps, taps, bias_all, sbias, dlog,
        scratch=[pltpu.VMEM((T + 8, XBC), F32)],
    )
    heads = MH // seqs
    ends = cum[T - 1, :MH]
    high = ends.astype(BF)
    low = (ends - high.astype(F32)).astype(BF)
    extra = jnp.concatenate([high[:, None, None], low[:, None, None]], axis=1)
    extra = jnp.broadcast_to(jnp.pad(extra, ((0, 0), (0, 14), (0, 0))), (MH, 16, NST))
    packed = jnp.concatenate([fresh.reshape(MH, AP, NST), extra], axis=1)
    packed = lax.all_to_all(
        packed.reshape(seqs, heads, AP + 16, NST), "seq", split_axis=0, concat_axis=0, tiled=True
    )
    states, totals = state_scan(packed, seqs)
    running = jnp.zeros_like(states[0])
    starts = []
    for c in range(seqs):
        starts.append(running.astype(BF))
        running = running * totals[c][:, None, None] + states[c]
    starts = lax.all_to_all(
        jnp.stack(starts), "seq", split_axis=0, concat_axis=0, tiled=True
    ).reshape(D_SSM, NST)
    attn_tok, lse = call(
        functools.partial(attend_forward, "seq"),
        [((T, QH * AP), BF), ((QH, T), F32)],
        query_rot, kv_all,
        scratch=[pltpu.VMEM((QH * AP, T), F32), pltpu.VMEM((QH, T), F32), pltpu.VMEM((QH, T), F32)],
    )
    (mixed_y,) = call(mamba_second, [((T, D_SSM), BF)], act, dt, cum, starts, skip)

    proj_gate = tail[:, :width].reshape(-1, FF)
    proj_up = tail[:, width : 2 * width].reshape(-1, FF)
    low_rows = 2 * width
    out_mixer = tail[:, low_rows : low_rows + mix_rows, :1024].reshape(-1, 1024)
    out_attn = tail[:, low_rows + mix_rows :, :1024].reshape(-1, 1024)
    proj_down = tail[:, low_rows:, 1024:].reshape(-1, 1024)
    mixed = mixed_y.astype(F32)
    gated = mixed * jax.nn.silu(gate_pre)
    scale_two = rms_scale(gated)
    normed_two = gated * scale_two
    normed_mix = (normed_two * gain_gated).astype(BF)
    middle = resid + dot(normed_mix, out_mixer) + dot(attn_tok, out_attn)
    scale_three = rms_scale(middle)
    normed_three = middle * scale_three
    normed_ffn = (normed_three * gain_ffn).astype(BF)
    gate_half = dot(normed_ffn, proj_gate)
    up_half = dot(normed_ffn, proj_up)
    activ = (jax.nn.silu(gate_half) * up_half).astype(BF)
    block_out = (middle + dot(activ, proj_down)).astype(BF)

    ograd = out_grad[0]
    grad_activ = dot(ograd, proj_down, NT)
    grad_down = dot(activ, ograd, TN).astype(BF)
    grad_g = (grad_activ * up_half * silu_slope(gate_half)).astype(BF)
    grad_u = (grad_activ * jax.nn.silu(gate_half)).astype(BF)
    grad_gw = dot(normed_ffn, grad_g, TN).astype(BF)
    grad_uw = dot(normed_ffn, grad_u, TN).astype(BF)
    grad_nffn = dot(grad_g, proj_gate, NT) + dot(grad_u, proj_up, NT)
    grad_ffn = jnp.sum(grad_nffn * normed_three, axis=0)
    grad_middle = ograd.astype(F32) + rms_back(grad_nffn * gain_ffn, normed_three, scale_three)
    middle_bf = grad_middle.astype(BF)
    grad_mixed = dot(normed_mix, middle_bf, TN).astype(BF)
    grad_attended = dot(attn_tok, middle_bf, TN).astype(BF)
    grad_nmix = dot(middle_bf, out_mixer, NT)
    grad_otok = dot(middle_bf, out_attn, NT).astype(BF)
    grad_gated = jnp.sum(grad_nmix * normed_two, axis=0)
    grad_gz = rms_back(grad_nmix * gain_gated, normed_two, scale_two)
    grad_ymix = (grad_gz * jax.nn.silu(gate_pre)).astype(BF)
    grad_gate = (grad_gz * mixed * silu_slope(gate_pre)).astype(BF)
    tail_grad = jnp.concatenate(
        [
            grad_gw.reshape(shards, width, FF),
            grad_uw.reshape(shards, width, FF),
            jnp.concatenate(
                [
                    jnp.concatenate(
                        [
                            grad_mixed.reshape(shards, mix_rows, 1024),
                            grad_attended.reshape(shards, att_rows, 1024),
                        ],
                        axis=1,
                    ),
                    grad_down.reshape(shards, down_rows, 1024),
                ],
                axis=2,
            ),
        ],
        axis=1,
    )
    tail_piece = lax.psum_scatter(tail_grad, "fsdp", scatter_dimension=0, tiled=True)[0]

    (dstart,) = call(mamba_back_first, [((D_SSM, NST), BF)], grad_ymix, act, cum)
    dstarts = lax.all_to_all(
        dstart.reshape(seqs, heads, AP, NST), "seq", split_axis=0, concat_axis=0, tiled=True
    ).astype(F32)
    running = jnp.zeros_like(dstarts[0])
    dends = [None] * seqs
    for c in reversed(range(seqs)):
        dends[c] = running.astype(BF)
        running = running * totals[c][:, None, None] + dstarts[c]
    dends = lax.all_to_all(
        jnp.stack(dends), "seq", split_axis=0, concat_axis=0, tiled=True
    ).reshape(D_SSM, NST)
    dq, dkv = call(
        functools.partial(attend_backward, "seq"),
        [((T, QH * AP), F32), ((kv_all.shape[0], 2 * KVH * AP), BF)],
        query_rot, kv_all, attn_tok, lse, grad_otok,
    )
    dkv = lax.psum_scatter(dkv, "seq", scatter_dimension=0, tiled=True)
    qgrad = (dq * cos_q - swap_halves(dq) * sin_q).astype(BF)
    dk = dkv[:, : KVH * AP].astype(F32)
    kgrad = (dk * cos_k - swap_halves(dk) * sin_k).astype(BF)
    dconv, dtaps, dbias, dsteps, dhead = call(
        mamba_back_second,
        [((T, XBC), F32), ((8, XBC), F32), ((8, XBC), F32), ((T, 128), BF), ((8, 128), F32)],
        grad_ymix, xbc, halo, act, dt, cum, starts, dends, steps, taps, bias_all, sbias, dlog, skip,
        scratch=[pltpu.VMEM((T + 8, XBC), F32), pltpu.VMEM((T, XBC), F32)],
    )
    ahead = lax.ppermute(dconv[:8].astype(BF), "seq", [(i + 1, i) for i in range(seqs - 1)])
    later = jnp.concatenate([dconv, ahead.astype(F32)], axis=0)
    du = taps[3:4] * dconv
    for lag in range(3):
        du = du + taps[lag : lag + 1] * later[3 - lag : 3 - lag + T]
    grad_proj = jnp.concatenate(
        [grad_gate, du.astype(BF), qgrad, kgrad, dkv[:, KVH * AP :], dsteps], axis=1
    )

    grad_front = dot(normed_in, grad_proj, TN).astype(BF)
    grad_nin = dot(grad_proj, front, NT)
    grad_norm = jnp.sum(grad_nin * normed_one, axis=0)
    input_grad = grad_middle + rms_back(grad_nin * gain_one, normed_one, scale_one)
    front_piece = lax.psum_scatter(grad_front, "fsdp", scatter_dimension=0, tiled=True)
    front_sum, tail_sum = lax.psum((front_piece, tail_piece), "seq")
    vectors = jnp.concatenate(
        [
            grad_norm, grad_ffn, grad_gated, dbias[0], dtaps[:4].reshape(-1),
            dhead[0, :MH], dhead[1, :MH], dhead[2, :MH],
        ]
    )
    vectors = lax.psum(vectors, ("seq", "fsdp"))
    pos = lax.axis_index("fsdp")

    def own(start, size, full):
        return lax.dynamic_slice_in_dim(vectors[start : start + full], pos * size, size, 0)

    at = 0
    owned = []
    for size, full in ((width, 1024), (width, 1024), (gated_gain.shape[0], D_SSM), (kernel_size, XBC)):
        owned.append(own(at, size, full))
        at += full
    own_taps = jnp.stack([own(at + lag * XBC, kernel_size, XBC) for lag in range(4)], axis=1)
    at += 4 * XBC
    tail_sum = tail_sum.astype(F32)
    front_sum = front_sum.astype(F32)
    return (
        block_out[None],
        input_grad[None],
        owned[0],
        jnp.concatenate([front_sum[:, : D_SSM + XBC], front_sum[:, 4096:4120]], axis=1),
        front_sum[:, 3328:4096],
        own_taps,
        owned[3],
        vectors[at : at + MH],
        vectors[at + MH : at + 2 * MH],
        vectors[at + 2 * MH : at + 3 * MH],
        owned[2],
        tail_sum[low_rows : low_rows + mix_rows, :1024],
        tail_sum[low_rows + mix_rows :, :1024],
        owned[1],
        jnp.concatenate([tail_sum[:width], tail_sum[width : 2 * width]], axis=1),
        tail_sum[low_rows:, 1024:],
    )


def solution(mesh):
    tokens = P("fsdp", "seq", None)
    vector = P("fsdp")
    matrix = P("fsdp", None)
    in_specs = (
        tokens, vector, matrix, matrix, matrix, vector, P(), P(), P(), vector, matrix, matrix, vector,
        matrix, matrix, tokens,
    )
    out_specs = (
        tokens, tokens, vector, matrix, matrix, matrix, vector, P(), P(), P(), vector, matrix, matrix,
        vector, matrix, matrix,
    )
    return jax.shard_map(
        functools.partial(per_device, mesh.shape["seq"]),
        mesh=mesh, in_specs=in_specs, out_specs=out_specs, check_vma=False,
    )
```

time: 1380 us -> 755 us (0.55)
  waiting for transfers between devices: 625 us -> 403 us
  blocking collectives: 255 us -> 75 us
  matrix products: 217 us -> 49.9 us
  other arithmetic: 115 us -> 53.1 us
  Pallas kernels: 0 us -> 33 us
  local copies, waits for them, and re-layouts: 101 us -> 76 us
    reduce_scatter x8 -> x3, waiting for transfers between devices: 442 us -> 146 us  [the longest x1 146 us: per_device(): lax.psum_scatter(tail_grad, 'fsdp', scatter_dimension=0, tiled=True)[0]]
    dot_general x58 -> x18, matrix products: 217 us -> 49.9 us  [dot(): lax.dot_general(a, b, dims, preferred_element_type=F32, precision=precision)]
    unnamed x2 -> x0, blocking collectives: 136 us -> none
    psum x1, waiting for transfers between devices: 0.01 us -> 83.9 us  [per_device(): front_sum, tail_sum = lax.psum((front_piece, tail_piece), 'seq')]
    pallas_call x0 -> x6, Pallas kernels: none -> 33 us  [call(): pl.pallas_call(kernel, out_shape=[jax.ShapeDtypeStruct(shape, dtype) for...]
    dynamic_update_slice x32 -> x0, local copies, waits for them, and re-layouts: 25.9 us -> none  [the longest x8 15 us: per_device(): lax.scan(backward_block, (empty, empty), (query_rot.reshape(count, block,...]
    reduce_sum x22 -> x0, other arithmetic: 25.4 us -> none  [the longest x2 10.7 us: conv_apply(): result = result + kernel[:, lag][None, :] * padded[lag:lag + length]]
    all_to_all x9 -> x4, waiting for transfers between devices: 38.5 us -> 18.2 us  [the longest x1 11.8 us: per_device(): lax.all_to_all(packed.reshape(seqs, heads, AP + 16, NST), 'seq', split_ax...]
  transfers between devices with their start and end apart: 27 -> 13, of which waited for: 15 -> 7; matrix products, arithmetic and copies ran while one was open for 29% -> 12% of each run, Pallas kernels for 0% -> 4%
where the time goes in v1:
time: 755 us; the launch traced here: 746 us
  waiting for transfers between devices  403 us (53%)
  local copies, waits for them, and re-layouts  76 us (10%)
  blocking collectives  75 us (10%)
  other arithmetic  53.1 us (7%)
  matrix products  49.9 us (7%)
  starting transfers between devices  40.5 us (5%)
  Pallas kernels  33 us (4%)
  between operations  15.8 us (2%)
    reduce_scatter x1, waiting for transfers between devices, per_device(): lax.psum_scatter(tail_grad, 'fsdp', scatter_dimension=0, tiled=True)[0]  146 us
    psum x1, waiting for transfers between devices, per_device(): front_sum, tail_sum = lax.psum((front_piece, tail_piece), 'seq')  83.9 us
    all_gather x1, waiting for transfers between devices, per_device(): tail = lax.all_gather(tail_shard, 'fsdp', axis=0, tiled=False)  78.2 us
    all_gather x1, waiting for transfers between devices, per_device(): front = lax.all_gather(front_shard, 'fsdp', axis=0, tiled=True)  76.1 us
    psum x1, blocking collectives, per_device(): vectors = lax.psum(vectors, ('seq', 'fsdp'))  75 us
    dot_general x18, matrix products, dot(): lax.dot_general(a, b, dims, preferred_element_type=F32, precision=precision)  49.9 us
    pallas_call x6, Pallas kernels, call(): pl.pallas_call(kernel, out_shape=[jax.ShapeDtypeStruct(shape, dtype) for...  33 us
    unnamed x242, local copies, waits for them, and re-layouts  24.1 us
  transfers between devices with their start and end apart: 13, of which 7 were waited for; matrix products, arithmetic and copies ran while one was open for 12% of the time, Pallas kernels for 4%

profile of v1, /device:TPU:0, one launch (start us, length us, event | category | flops | bytes accessed | tf_op | source)
XLA Modules:
  0.0 745.9 jit_solution(2578487850148403848)
XLA Ops:
  9.8 2.8 concatenate.57
  15.2 76.1 %all-gather.5.cloned.1.call-done = bf16[1024,4224]{1,0:T(8,128)(2,1)} async-done(((bf16[64,4224]{1,0:T(8,128)(2,1)}), bf16[1024,4224]{1,0:T(8,128)(2,1)}) %all-gather.5.cloned.1.call-update) | async-done | bytes 8650768 | tf_op jit(solution)/shard_map/all_gather | solution.py:342
  93.5 8.0 %fusion.58 = (bf16[256,4224]{1,0:T(8,128)(2,1)S(1)}, f32[256,4224]{1,0:T(8,128)}) fusion(bf16[1024,4224]{1,0:T(8,128)(2,1)} %all-gather.5.cloned.1.call-done, bf16[1,256,1024]{2,1,0:T(8,128)(2,1)S(1)} %copy-done.46, f32[1024]{0:T(1024)S(1)} %reshape.330, f32[256]{0:T(256)S(1)} %add_rsqrt_fusion.2), kind=kOutput, calls=%fused_computation.177 | convolution fusion | flops 2216722432 | bytes 15668224 | tf_op jit(solution)/shard_map/dot_general | solution.py:31
  107.2 2.5 collective-permute-start
  113.6 3.4 shard_map.279
  118.5 6.5 all-to-all-start
  127.5 11.8 %all-to-all-done = bf16[8,3,80,128]{3,2,1,0:T(8,128)(2,1)} async-done(((bf16[8,3,80,128]{3,2,1,0:T(8,128)(2,1)}), bf16[8,3,80,128]{3,2,1,0:T(8,128)(2,1)}, u32[]{:S(2)}, u32[]{:S(2)}) %all-to-all-start) | async-done | bytes 491552 | tf_op jit(solution)/shard_map/all_to_all | solution.py:399
  146.9 3.6 all-to-all-start.1
  158.6 2.3 add_convert_fusion.q
  164.5 4.6 shard_map.280
  173.8 2.6 shard_map.281
  177.1 78.2 %all-gather.9.cloned.1.call-done = bf16[4096,2048]{1,0:T(8,128)(2,1)} async-done(((bf16[256,2048]{1,0:T(8,128)(2,1)}), bf16[4096,2048]{1,0:T(8,128)(2,1)}) %all-gather.9.cloned.1.call-update) | async-done | bytes 16777232 | tf_op jit(solution)/shard_map/all_gather | solution.py:352
  256.6 2.6 slice.385
  259.2 2.8 slice.393
  262.1 5.8 fusion.51
  272.6 3.0 multiply_convert_fusion
  286.3 4.4 all-to-all-start.2
  292.7 3.2 shard_map.284
  307.1 21.5 %all-to-all-start.3 = ((bf16[8,3,64,128]{3,2,1,0:T(8,128)(2,1)}), bf16[8,3,64,128]{3,2,1,0:T(8,128)(2,1)S(1)}, u32[]{:S(2)}, u32[]{:S(2)}) async-start(bf16[8,3,64,128]{3,2,1,0:T(8,128)(2,1)} %constant_dynamic-update-slice_fusion.1), calls=%async_computation.3 | async-start | bytes 786432 | tf_op jit(solution)/shard_map/all_to_all | solution.py:489
  335.5 4.2 all-to-all-done.3
  344.6 17.4 %shard_map.283 = (f32[256,1792]{1,0:T(8,128)S(1)}, f32[8,1792]{1,0:T(8,128)S(1)}, f32[8,1792]{1,0:T(8,128)S(1)}, bf16[256,128]{1,0:T(8,128)(2,1)S(1)}, f32[8,128]{1,0:T(8,128)S(1)}) custom-call(bf16[256,1536]{1,0:T(8,128)(2,1)S(1)} %copy-done.2, bf16[256,1792]{1,0:T(8,128)(2,1)S(1)} %slice.361.xbc, bf16[8,1792]{1,0:T(8,128)(2,1)S(1)} %copy-done.31, ...), custom_call_target="tpu_custom_call" | custom-call | tf_op jit(solution)/shard_map/pallas_call | solution.py:289
  363.6 3.4 fusion.28
  368.4 5.2 fusion.27
  379.4 7.6 %convolution_convert_fusion = bf16[1024,4224]{1,0:T(8,128)(2,1)} fusion(bf16[256,4224]{1,0:T(8,128)(2,1)} %constant_dynamic-update-slice_fusion.2, bf16[1,256,1024]{2,1,0:T(8,128)(2,1)S(1)} %copy-done.48, f32[1024]{0:T(1024)S(1)} %copy-done.79, f32[256]{0:T(256)S(1)} %copy-done.90), kind=kOutput, calls=%fused_computation.1 | convolution fusion | flops 2219966464 | bytes 11342848 | tf_op jit(solution)/shard_map/dot_general | solution.py:31
  393.3 2.8 convolution_convert_fusion.1
  396.1 7.1 maximum_maximum_fusion
  405.0 4.7 fusion.18
  411.4 7.8 %fusion.25 = (f32[1024]{0:T(1024)S(1)}, f32[256]{0:T(256)S(1)}, f32[256,1024]{1,0:T(8,128)}) fusion(bf16[1,256,1024]{2,1,0:T(8,128)(2,1)S(1)} %copy-done.48, f32[256]{0:T(256)S(1)} %copy-done.90, f32[1024]{0:T(1024)S(1)} %copy-done.79, bf16[256,4224]{1,0:T(8,128)(2,1)} %constant_dynamic-update-slice_fusion.2, ...), kind=kOutput, calls=%fused_computation.56 | convolution fusion | flops 2216426240 | bytes 12396544 | tf_op jit(solution)/shard_map/dot_general | solution.py:31
  419.3 75.0 %psum.21 = f32[12616]{0:T(1024)S(1)} all-reduce(f32[12616]{0:T(1024)S(1)} %concatenate.70), channel_id=1, replica_groups=mesh['seq'=8,'fsdp'=16] {'seq','fsdp'}, use_global_device_ids=true, to_apply=%region_10.11 | all-reduce | flops 12616 | bytes 100928 | tf_op jit(solution)/shard_map/psum | solution.py:528
  496.1 146.0 %reduce-scatter.8.cloned.1.call-done = bf16[1,256,2048]{2,1,0:T(8,128)(2,1)} async-done(((bf16[16,256,2048]{2,1,0:T(8,128)(2,1)}), bf16[1,256,2048]{2,1,0:T(8,128)(2,1)}) %reduce-scatter.8.cloned.1.call-update) | async-done | bytes 1048592 | tf_op jit(solution)/shard_map/reduce_scatter | solution.py:478
  644.3 2.8 fusion.24
  647.1 83.9 %all-reduce.9.cloned.1.call-done = (bf16[64,4224]{1,0:T(8,128)(2,1)}, bf16[256,2048]{1,0:T(8,128)(2,1)}) async-done(((bf16[64,4224]{1,0:T(8,128)(2,1)}, bf16[256,2048]{1,0:T(8,128)(2,1)}), (bf16[64,4224]{1,0:T(8,128)(2,1)}, bf16[256,2048]{1,0:T(8,128)(2,1)})) %all-reduce.9.cloned.1.call-update) | async-done | bytes 1589264 | tf_op jit(solution)/shard_map/psum | solution.py:521
  (407 shorter events, 116.3 us)
Async XLA Ops:
  7.2 84.1 %all-gather.5.cloned.1.call-start = ((), (), s32[]{:S(2)}) async-start(), calls=%async_computation.7 | async-start | bytes 9191424 | tf_op jit(solution)/shard_map/all_gather | solution.py:342
  14.4 157.2 %all-gather.7.cloned.1.call-start = ((), (), s32[]{:S(2)}) async-start(), calls=%async_computation.8 | async-start | bytes 1179648 | tf_op jit(solution)/shard_map/all_gather | solution.py:384
  14.8 87.0 %copy-start.71 = (f32[256,128]{1,0:T(8,128)}, f32[256,128]{1,0:T(8,128)S(1)}, u32[]{:S(2)}) copy-start(f32[256,128]{1,0:T(8,128)S(1)} %copy.88) | copy-start | bytes 393220
  15.0 86.8 %copy-start.73 = (f32[256,128]{1,0:T(8,128)}, f32[256,128]{1,0:T(8,128)S(1)}, u32[]{:S(2)}) copy-start(f32[256,128]{1,0:T(8,128)S(1)} %copy.91) | copy-start | bytes 393220
  15.2 86.3 %copy-start.89 = (f32[256]{0:T(256)}, f32[256]{0:T(256)S(1)}, u32[]{:S(2)}) copy-start(f32[256]{0:T(256)S(1)} %add_rsqrt_fusion.2) | copy-start | bytes 3076
  102.5 152.8 %all-gather.9.cloned.1.call-start = ((), (), s32[]{:S(2)}) async-start(), calls=%async_computation.12 | async-start | bytes 17825792 | tf_op jit(solution)/shard_map/all_gather | solution.py:352
  107.2 5.0 collective-permute-start
  112.3 29.7 %copy-start.27 = (f32[8,1792]{1,0:T(8,128)}, f32[8,1792]{1,0:T(8,128)S(1)}, u32[]{:S(2)}) copy-start(f32[8,1792]{1,0:T(8,128)S(1)} %pad.23.taps) | copy-start | bytes 172036
  117.0 25.6 %copy-start.17 = (f32[256,128]{1,0:T(8,128)}, f32[256,128]{1,0:T(8,128)S(1)}, u32[]{:S(2)}) copy-start(f32[256,128]{1,0:T(8,128)S(1)} %get-tuple-element.32.cum) | copy-start | bytes 393220
  117.1 25.6 %copy-start.24 = (f32[256,128]{1,0:T(8,128)}, f32[256,128]{1,0:T(8,128)S(1)}, u32[]{:S(2)}) copy-start(f32[256,128]{1,0:T(8,128)S(1)} %get-tuple-element.31.dt) | copy-start | bytes 393220
  117.1 166.4 %copy-start = (f32[256,1792]{1,0:T(8,128)}, f32[256,1792]{1,0:T(8,128)S(1)}, u32[]{:S(2)}) copy-start(f32[256,1792]{1,0:T(8,128)S(1)} %get-tuple-element.30.act) | copy-start | bytes 5505028
  118.5 20.8 %all-to-all-start = ((bf16[8,3,80,128]{3,2,1,0:T(8,128)(2,1)}), bf16[8,3,80,128]{3,2,1,0:T(8,128)(2,1)}, u32[]{:S(2)}, u32[]{:S(2)}) async-start(bf16[8,3,80,128]{3,2,1,0:T(8,128)(2,1)} %pad_maximum_fusion.3), calls=%async_computation | async-start | bytes 983040 | tf_op jit(solution)/shard_map/all_to_all | solution.py:399
  125.0 36.6 %copy-start.40 = (f32[1,128]{1,0:T(1,128)}, f32[1,128]{1,0:T(1,128)S(1)}, u32[]{:S(2)}) copy-start(f32[1,128]{1,0:T(1,128)S(1)} %pad_bitcast_fusion.skip) | copy-start | bytes 1540
  127.5 24.4 %copy-start.95 = (f32[16,64]{1,0:T(8,128)S(1)}, f32[16,64]{1,0:T(8,128)}, u32[]{:S(2)}) copy-start(f32[16,64]{1,0:T(8,128)} %get-tuple-element.82) | copy-start | bytes 12292
  146.9 14.0 %all-to-all-start.1 = ((bf16[8,3,64,128]{3,2,1,0:T(8,128)(2,1)}), bf16[8,3,64,128]{3,2,1,0:T(8,128)(2,1)S(1)}, u32[]{:S(2)}, u32[]{:S(2)}) async-start(bf16[8,3,64,128]{3,2,1,0:T(8,128)(2,1)} %fusion.42), calls=%async_computation.1 | async-start | bytes 786432 | tf_op jit(solution)/shard_map/all_to_all | solution.py:408
  286.3 13.6 %all-to-all-start.2 = ((bf16[8,3,64,128]{3,2,1,0:T(8,128)(2,1)}), bf16[8,3,64,128]{3,2,1,0:T(8,128)(2,1)}, u32[]{:S(2)}, u32[]{:S(2)}) async-start(bf16[8,3,64,128]{3,2,1,0:T(8,128)(2,1)} %bitcast.125), calls=%async_computation.2 | async-start | bytes 786432 | tf_op jit(solution)/shard_map/all_to_all | solution.py:481
  290.8 83.9 %reduce-scatter.4.cloned.1.call-start = ((), (), s32[]{:S(2)}) async-start(), calls=%async_computation.9 | async-start | bytes 1179648 | tf_op jit(solution)/shard_map/reduce_scatter | solution.py:497
  297.8 41.9 %copy-start.2 = (bf16[256,1536]{1,0:T(8,128)(2,1)S(1)}, bf16[256,1536]{1,0:T(8,128)(2,1)}, u32[]{:S(2)}) copy-start(bf16[256,1536]{1,0:T(8,128)(2,1)} %copy-done.1) | copy-start | bytes 2359300
  297.8 41.9 %copy-start.7 = (bf16[8,3,64,128]{3,2,1,0:T(8,128)(2,1)S(1)}, bf16[8,3,64,128]{3,2,1,0:T(8,128)(2,1)}, u32[]{:S(2)}) copy-start(bf16[8,3,64,128]{3,2,1,0:T(8,128)(2,1)} %copy-done.5) | copy-start | bytes 1179652
  297.8 41.9 %copy-start.37 = (f32[1,128]{1,0:T(1,128)S(1)}, f32[1,128]{1,0:T(1,128)}, u32[]{:S(2)}) copy-start(f32[1,128]{1,0:T(1,128)} %copy-done.36) | copy-start | bytes 1540
  297.8 41.9 %copy-start.39 = (f32[1,128]{1,0:T(1,128)S(1)}, f32[1,128]{1,0:T(1,128)}, u32[]{:S(2)}) copy-start(f32[1,128]{1,0:T(1,128)} %copy-done.38) | copy-start | bytes 1540
  307.1 32.6 %all-to-all-start.3 = ((bf16[8,3,64,128]{3,2,1,0:T(8,128)(2,1)}), bf16[8,3,64,128]{3,2,1,0:T(8,128)(2,1)S(1)}, u32[]{:S(2)}, u32[]{:S(2)}) async-start(bf16[8,3,64,128]{3,2,1,0:T(8,128)(2,1)} %constant_dynamic-update-slice_fusion.1), calls=%async_computation.3 | async-start | bytes 786432 | tf_op jit(solution)/shard_map/all_to_all | solution.py:489
  328.6 167.5 %reduce-scatter.6.cloned.1.call-start = ((), (), s32[]{:S(2)}) async-start(), calls=%async_computation.10 | async-start | bytes 9191424 | tf_op jit(solution)/shard_map/reduce_scatter | solution.py:520
  344.6 19.0 %copy-start.103 = (f32[256]{0:T(256)S(1)}, f32[256]{0:T(256)}, u32[]{:S(2)}) copy-start(f32[256]{0:T(256)} %copy-done.102) | copy-start | bytes 3076
  362.2 6.2 collective-permute-start.1
  387.0 255.1 %reduce-scatter.8.cloned.1.call-start = ((), (), s32[]{:S(2)}) async-start(), calls=%async_computation.11 | async-start | bytes 17825792 | tf_op jit(solution)/shard_map/reduce_scatter | solution.py:478
  403.3 327.8 %all-reduce.9.cloned.1.call-start = ((), (), s32[]{:S(2)}) async-start(), calls=%async_computation.13 | async-start | bytes 3178496 | tf_op jit(solution)/shard_map/psum | solution.py:521
  411.4 232.9 %copy-start.83 = (f32[1024]{0:T(1024)S(1)}, f32[1024]{0:T(1024)}, u32[]{:S(2)}) copy-start(f32[1024]{0:T(1024)} %reshape.333) | copy-start | bytes 12292
  411.4 232.9 %copy-start.88 = (f32[256]{0:T(256)S(1)}, f32[256]{0:T(256)}, u32[]{:S(2)}) copy-start(f32[256]{0:T(256)} %copy-done.87) | copy-start | bytes 3076
  411.4 232.9 %copy-start.98 = (f32[256]{0:T(256)S(1)}, f32[256]{0:T(256)}, u32[]{:S(2)}) copy-start(f32[256]{0:T(256)} %copy-done.97) | copy-start | bytes 3076
  419.2 225.1 %copy-start.51 = (f32[256,1024]{1,0:T(8,128)S(1)}, f32[256,1024]{1,0:T(8,128)}, u32[]{:S(2)}) copy-start(f32[256,1024]{1,0:T(8,128)} %copy-done.50) | copy-start | bytes 3145732
  419.2 225.1 %copy-start.59 = (bf16[1,256,1024]{2,1,0:T(8,128)(2,1)S(1)}, bf16[1,256,1024]{2,1,0:T(8,128)(2,1)}, u32[]{:S(2)}) copy-start(bf16[1,256,1024]{2,1,0:T(8,128)(2,1)} %param.31) | copy-start | bytes 1572868
  (100 other events, 457.5 us)
Sparse Core Ops, SparseCore 0:
  14.5 76.7 all-gather.4
  102.7 41.2 all-gather.6
  147.0 108.3 all-gather.8
  297.9 60.4 reduce-scatter.3
  387.1 105.0 reduce-scatter.5
  496.4 145.6 reduce-scatter.7
  644.8 86.2 all-reduce.8

commit v2 on v1

--- a/solution.py
+++ b/solution.py
@@ -315,6 +315,20 @@
     return jnp.pad(value.astype(F32), (0, 128 - value.shape[0]))[None, :]
 
 
+def exchange(value):
+    return lax.all_to_all(value, "seq", split_axis=0, concat_axis=0, tiled=True)
+
+
+def share(value, seqs):
+    return exchange(jnp.broadcast_to(value[None], (seqs,) + value.shape))
+
+
+def sum_over(value, seqs):
+    rows, cols = value.shape
+    parts = exchange(value.reshape(seqs, rows // seqs, cols))
+    return share(jnp.sum(parts.astype(F32), axis=0).astype(BF), seqs).reshape(rows, cols)
+
+
 def state_scan(packed, seqs):
     states = packed[:, :, :AP, :].astype(F32)
     logs = packed[:, :, AP, 0].astype(F32) + packed[:, :, AP + 1, 0].astype(F32)
@@ -381,7 +395,7 @@
     key_rot = (keys * cos_k + swap_halves(keys) * sin_k).astype(BF)
     kv_own = jnp.concatenate([key_rot, keyvals[:, KVH * AP :]], axis=1)
     halo = lax.ppermute(xbc[-8:], "seq", [(i, i + 1) for i in range(seqs - 1)])
-    kv_all = lax.all_gather(kv_own, "seq", axis=0, tiled=True)
+    kv_all = share(kv_own, seqs).reshape(seqs * T, 2 * KVH * AP)
     sbias, dlog, skip = pad_lanes(step_bias), pad_lanes(decay_log), pad_lanes(skip_gain)
     act, dt, cum, fresh = call(
         mamba_first,
@@ -494,7 +508,8 @@
         [((T, QH * AP), F32), ((kv_all.shape[0], 2 * KVH * AP), BF)],
         query_rot, kv_all, attn_tok, lse, grad_otok,
     )
-    dkv = lax.psum_scatter(dkv, "seq", scatter_dimension=0, tiled=True)
+    dkv = exchange(dkv.reshape(seqs, T, 2 * KVH * AP))
+    dkv = jnp.sum(dkv.astype(F32), axis=0).astype(BF)
     qgrad = (dq * cos_q - swap_halves(dq) * sin_q).astype(BF)
     dk = dkv[:, : KVH * AP].astype(F32)
     kgrad = (dk * cos_k - swap_halves(dk) * sin_k).astype(BF)
@@ -517,8 +532,9 @@
     grad_nin = dot(grad_proj, front, NT)
     grad_norm = jnp.sum(grad_nin * normed_one, axis=0)
     input_grad = grad_middle + rms_back(grad_nin * gain_one, normed_one, scale_one)
+    grad_front, tail_piece = lax.optimization_barrier((grad_front, tail_piece))
     front_piece = lax.psum_scatter(grad_front, "fsdp", scatter_dimension=0, tiled=True)
-    front_sum, tail_sum = lax.psum((front_piece, tail_piece), "seq")
+    front_sum, tail_sum = sum_over(front_piece, seqs), sum_over(tail_piece, seqs)
     vectors = jnp.concatenate(
         [
             grad_norm, grad_ffn, grad_gated, dbias[0], dtaps[:4].reshape(-1),

time: 755 us -> 570 us (0.75)
  waiting for transfers between devices: 403 us -> 185 us
  starting transfers between devices: 40.5 us -> 62.2 us
  blocking collectives: 75 us -> 90.8 us
    reduce_scatter x1, waiting for transfers between devices: 146 us -> 41.8 us  [per_device(): lax.psum_scatter(tail_grad, 'fsdp', scatter_dimension=0, tiled=True)[0]]
    psum x1 -> x0, waiting for transfers between devices: 83.9 us -> none  [per_device(): front_sum, tail_sum = lax.psum((front_piece, tail_piece), 'seq')]
    all_gather x1, waiting for transfers between devices: 78.2 us -> 24.6 us  [per_device(): tail = lax.all_gather(tail_shard, 'fsdp', axis=0, tiled=False)]
    all_to_all x1 -> x6, starting transfers between devices: 4.43 us -> 42.9 us  [exchange(): return lax.all_to_all(value, 'seq', split_axis=0, concat_axis=0, tiled=True)]
    all_to_all x1 -> x6, waiting for transfers between devices: 2.16 us -> 31.8 us  [exchange(): return lax.all_to_all(value, 'seq', split_axis=0, concat_axis=0, tiled=True)]
    all_to_all x1, starting transfers between devices: 21.5 us -> 4.09 us  [per_device(): lax.all_to_all(jnp.stack(dends), 'seq', split_axis=0, concat_axis=0, tile...]
    all_to_all x0 -> x1, blocking collectives: none -> 13.8 us  [per_device(): lax.all_to_all(dstart.reshape(seqs, heads, AP, NST), 'seq', split_axis=0,...]
    all_to_all x1, waiting for transfers between devices: 0.01 us -> 10.7 us  [per_device(): lax.all_to_all(jnp.stack(starts), 'seq', split_axis=0, concat_axis=0, til...]
  transfers between devices with their start and end apart: 13 -> 15, of which waited for: 7 -> 10; matrix products, arithmetic and copies ran while one was open for 12% -> 20% of each run, Pallas kernels for 4% -> 6%
where the time goes in v2:
time: 570 us; the launch traced here: 561 us
  waiting for transfers between devices  185 us (32%)
  blocking collectives  90.8 us (16%)
  local copies, waits for them, and re-layouts  72.5 us (13%)
  starting transfers between devices  62.2 us (11%)
  matrix products  50.5 us (9%)
  other arithmetic  49.4 us (9%)
  Pallas kernels  35.6 us (6%)
  between operations  15.6 us (3%)
    psum x1, blocking collectives, per_device(): vectors = lax.psum(vectors, ('seq', 'fsdp'))  77 us
    all_gather x1, waiting for transfers between devices, per_device(): front = lax.all_gather(front_shard, 'fsdp', axis=0, tiled=True)  72.8 us
    dot_general x18, matrix products, dot(): lax.dot_general(a, b, dims, preferred_element_type=F32, precision=precision)  50.5 us
    all_to_all x6, starting transfers between devices, exchange(): return lax.all_to_all(value, 'seq', split_axis=0, concat_axis=0, tiled=True)  42.9 us
    reduce_scatter x1, waiting for transfers between devices, per_device(): lax.psum_scatter(tail_grad, 'fsdp', scatter_dimension=0, tiled=True)[0]  41.8 us
    pallas_call x6, Pallas kernels, call(): pl.pallas_call(kernel, out_shape=[jax.ShapeDtypeStruct(shape, dtype) for...  35.6 us
    all_to_all x6, waiting for transfers between devices, exchange(): return lax.all_to_all(value, 'seq', split_axis=0, concat_axis=0, tiled=True)  31.8 us
    all_gather x1, waiting for transfers between devices, per_device(): tail = lax.all_gather(tail_shard, 'fsdp', axis=0, tiled=False)  24.6 us
  transfers between devices with their start and end apart: 15, of which 10 were waited for; matrix products, arithmetic and copies ran while one was open for 20% of the time, Pallas kernels for 6%

profile of v2, /device:TPU:0, one launch (start us, length us, event | category | flops | bytes accessed | tf_op | source)
XLA Modules:
  0.0 561.3 jit_solution(6260804656165869100)
XLA Ops:
  18.6 72.8 %all-gather.4.cloned.1.call-done = bf16[1024,4224]{1,0:T(8,128)(2,1)} async-done(((bf16[64,4224]{1,0:T(8,128)(2,1)}), bf16[1024,4224]{1,0:T(8,128)(2,1)}) %all-gather.4.cloned.1.call-update) | async-done | bytes 8650768 | tf_op jit(solution)/shard_map/all_gather | solution.py:356
  93.5 8.1 %fusion.58 = (bf16[256,4224]{1,0:T(8,128)(2,1)S(1)}, f32[256,4224]{1,0:T(8,128)}) fusion(bf16[1024,4224]{1,0:T(8,128)(2,1)} %all-gather.4.cloned.1.call-done, bf16[1,256,1024]{2,1,0:T(8,128)(2,1)S(1)} %copy-done.42, f32[1024]{0:T(1024)S(1)} %reshape.356, f32[256]{0:T(256)S(1)} %add_rsqrt_fusion.2), kind=kOutput, calls=%fused_computation.178 | convolution fusion | flops 2216722432 | bytes 15668224 | tf_op jit(solution)/shard_map/dot_general | solution.py:31
  106.1 3.4 shard_map.279
  112.0 7.2 %all-to-all-start = ((bf16[8,3,80,128]{3,2,1,0:T(8,128)(2,1)}), bf16[8,3,80,128]{3,2,1,0:T(8,128)(2,1)S(1)}, u32[]{:S(2)}, u32[]{:S(2)}) async-start(bf16[8,3,80,128]{3,2,1,0:T(8,128)(2,1)} %pad_maximum_fusion.3), calls=%async_computation | async-start | bytes 983040 | tf_op jit(solution)/shard_map/all_to_all | solution.py:413
  136.1 3.5 all-to-all-start.1
  142.2 10.7 %all-to-all-done.1 = bf16[8,3,64,128]{3,2,1,0:T(8,128)(2,1)S(1)} async-done(((bf16[8,3,64,128]{3,2,1,0:T(8,128)(2,1)}), bf16[8,3,64,128]{3,2,1,0:T(8,128)(2,1)S(1)}, u32[]{:S(2)}, u32[]{:S(2)}) %all-to-all-start.1) | async-done | bytes 393248 | tf_op jit(solution)/shard_map/all_to_all | solution.py:422
  154.1 4.3 all-to-all-start.2
  170.7 4.6 shard_map.280
  177.9 7.8 %all-to-all-done.2 = bf16[8,256,256]{2,1,0:T(8,128)(2,1)} async-done(((bf16[8,256,256]{2,1,0:T(8,128)(2,1)}), bf16[8,256,256]{2,1,0:T(8,128)(2,1)}, u32[]{:S(2)}, u32[]{:S(2)}) %all-to-all-start.2) | async-done | bytes 1048608 | tf_op jit(solution)/shard_map/all_to_all | solution.py:319
  186.6 3.8 shard_map.281
  191.1 24.6 %all-gather.6.cloned.1.call-done = bf16[4096,2048]{1,0:T(8,128)(2,1)} async-done(((bf16[256,2048]{1,0:T(8,128)(2,1)}), bf16[4096,2048]{1,0:T(8,128)(2,1)}) %all-gather.6.cloned.1.call-update) | async-done | bytes 16777232 | tf_op jit(solution)/shard_map/all_gather | solution.py:366
  219.7 3.9 slice.401
  223.7 6.0 %fusion.51 = (bf16[16,64,2048]{2,1,0:T(8,128)(2,1)S(1)}, bf16[16,64,2048]{2,1,0:T(8,128)(2,1)S(1)}) fusion(bf16[16,256,2048]{2,1,0:T(8,128)(2,1)} %bitcast.145), kind=kLoop, calls=%fused_computation.171 | loop fusion | bytes 16777216 | tf_op jit(solution)/shard_map/slice | solution.py:433
  246.5 6.7 %maximum_maximum_fusion = bf16[16,256,2048]{2,1,0:T(8,128)(2,1)} fusion(bf16[16,128,1024]{2,1,0:T(8,128)(2,1)S(1)} %bitcast.137, bf16[16,32,1024]{2,1,0:T(8,128)(2,1)S(1)} %bitcast.154, bf16[16,96,1024]{2,1,0:T(8,128)(2,1)S(1)} %bitcast.159, bf16[16,64,2048]{2,1,0:T(8,128)(2,1)S(1)} %bitcast.138, bf16[16,64,2048]{2,1,0:T(8,128)(2,1)S(1)} %bitcast.139), kind=kLoop, calls=%fused_computation | loop fusion | flops 83886080 | bytes 33554432 | tf_op jit(solution)/shard_map/concatenate | solution.py:472
  253.2 4.6 multiply_reduce_fusion
  262.7 13.8 %all_to_all.50 = bf16[8,3,64,128]{3,2,1,0:T(8,128)(2,1)S(1)} all-to-all(bf16[8,3,64,128]{3,2,1,0:T(8,128)(2,1)S(1)} %bitcast.134), channel_id=1, replica_groups=mesh['seq'=8,'fsdp'=16] {'seq'}, dimensions={0} | all-to-all | bytes 786432 | tf_op jit(solution)/shard_map/all_to_all | solution.py:495
  282.0 4.1 all-to-all-start.4
  290.3 4.6 shard_map.284
  296.7 23.5 %all-to-all-start.5 = ((bf16[8,256,256]{2,1,0:T(8,128)(2,1)}), bf16[8,256,256]{2,1,0:T(8,128)(2,1)}, u32[]{:S(2)}, u32[]{:S(2)}) async-start(bf16[8,256,256]{2,1,0:T(8,128)(2,1)} %bitcast.135), calls=%async_computation.5 | async-start | bytes 2097152 | tf_op jit(solution)/shard_map/all_to_all | solution.py:319
  325.7 17.5 %shard_map.283 = (f32[256,1792]{1,0:T(8,128)S(1)}, f32[8,1792]{1,0:T(8,128)S(1)}, f32[8,1792]{1,0:T(8,128)S(1)}, bf16[256,128]{1,0:T(8,128)(2,1)S(1)}, f32[8,128]{1,0:T(8,128)S(1)}) custom-call(bf16[256,1536]{1,0:T(8,128)(2,1)S(1)} %copy-done.2, bf16[256,1792]{1,0:T(8,128)(2,1)S(1)} %slice.369.xbc, bf16[8,1792]{1,0:T(8,128)(2,1)S(1)} %copy-done.28, ...), custom_call_target="tpu_custom_call" | custom-call | tf_op jit(solution)/shard_map/pallas_call | solution.py:289
  358.9 7.7 %convolution_convert_fusion = bf16[1024,4224]{1,0:T(8,128)(2,1)} fusion(bf16[256,4224]{1,0:T(8,128)(2,1)} %constant_dynamic-update-slice_fusion.2, bf16[1,256,1024]{2,1,0:T(8,128)(2,1)S(1)} %copy-done.44, f32[1024]{0:T(1024)S(1)} %copy-done.68, f32[256]{0:T(256)S(1)} %copy-done.83), kind=kOutput, calls=%fused_computation.1 | convolution fusion | flops 2219966464 | bytes 11342848 | tf_op jit(solution)/shard_map/dot_general | solution.py:31
  366.6 41.8 %reduce-scatter.3.cloned.1.call-done = bf16[1,256,2048]{2,1,0:T(8,128)(2,1)} async-done(((bf16[16,256,2048]{2,1,0:T(8,128)(2,1)}), bf16[1,256,2048]{2,1,0:T(8,128)(2,1)}) %reduce-scatter.3.cloned.1.call-update) | async-done | bytes 1048592 | tf_op jit(solution)/shard_map/reduce_scatter | solution.py:492
  409.9 4.3 fusion.18
  415.1 4.5 all-to-all-start.8
  419.6 8.6 %fusion.25 = (f32[1024]{0:T(1024)S(1)}, f32[256]{0:T(256)S(1)}, f32[256,1024]{1,0:T(8,128)}) fusion(bf16[1,256,1024]{2,1,0:T(8,128)(2,1)S(1)} %copy-done.44, f32[256]{0:T(256)S(1)} %copy-done.83, f32[1024]{0:T(1024)S(1)} %copy-done.68, bf16[256,4224]{1,0:T(8,128)(2,1)} %constant_dynamic-update-slice_fusion.2, ...), kind=kOutput, calls=%fused_computation.56 | convolution fusion | flops 2216426240 | bytes 12396544 | tf_op jit(solution)/shard_map/dot_general | solution.py:31
  428.3 77.0 %psum.7 = f32[12616]{0:T(1024)S(1)} all-reduce(f32[12616]{0:T(1024)S(1)} %concatenate.70), channel_id=1, replica_groups=mesh['seq'=8,'fsdp'=16] {'seq','fsdp'}, use_global_device_ids=true, to_apply=%region_10.11 | all-reduce | flops 12616 | bytes 100928 | tf_op jit(solution)/shard_map/psum | solution.py:544
  509.2 3.6 all-to-all-start.9
  517.1 7.7 %all-to-all-done.9 = bf16[8,32,2048]{2,1,0:T(8,128)(2,1)S(1)} async-done(((bf16[8,32,2048]{2,1,0:T(8,128)(2,1)}), bf16[8,32,2048]{2,1,0:T(8,128)(2,1)S(1)}, u32[]{:S(2)}, u32[]{:S(2)}) %all-to-all-start.9) | async-done | bytes 1048608 | tf_op jit(solution)/shard_map/all_to_all | solution.py:319
  527.4 3.5 all-to-all-start.6
  531.0 8.6 %all-to-all-done.6 = bf16[8,8,4224]{2,1,0:T(8,128)(2,1)S(1)} async-done(((bf16[8,8,4224]{2,1,0:T(8,128)(2,1)}), bf16[8,8,4224]{2,1,0:T(8,128)(2,1)S(1)}, u32[]{:S(2)}, u32[]{:S(2)}) %all-to-all-start.6) | async-done | bytes 540704 | tf_op jit(solution)/shard_map/all_to_all | solution.py:319
  540.5 3.5 all-to-all-start.7
  545.1 7.7 %all-to-all-done.7 = bf16[8,8,4224]{2,1,0:T(8,128)(2,1)S(1)} async-done(((bf16[8,8,4224]{2,1,0:T(8,128)(2,1)}), bf16[8,8,4224]{2,1,0:T(8,128)(2,1)S(1)}, u32[]{:S(2)}, u32[]{:S(2)}) %all-to-all-start.7) | async-done | bytes 540704 | tf_op jit(solution)/shard_map/all_to_all | solution.py:319
  (411 shorter events, 132.0 us)
Async XLA Ops:
  7.2 84.1 %all-gather.4.cloned.1.call-start = ((), (), s32[]{:S(2)}) async-start(), calls=%async_computation.12 | async-start | bytes 9191424 | tf_op jit(solution)/shard_map/all_gather | solution.py:356
  14.5 201.3 %all-gather.6.cloned.1.call-start = ((), (), s32[]{:S(2)}) async-start(), calls=%async_computation.15 | async-start | bytes 17825792 | tf_op jit(solution)/shard_map/all_gather | solution.py:366
  16.1 108.6 %copy-start.62 = (f32[256,128]{1,0:T(8,128)}, f32[256,128]{1,0:T(8,128)S(1)}, u32[]{:S(2)}) copy-start(f32[256,128]{1,0:T(8,128)S(1)} %copy.88) | copy-start | bytes 393220
  16.2 108.5 %copy-start.64 = (f32[256,128]{1,0:T(8,128)}, f32[256,128]{1,0:T(8,128)S(1)}, u32[]{:S(2)}) copy-start(f32[256,128]{1,0:T(8,128)S(1)} %copy.91) | copy-start | bytes 393220
  18.3 87.8 %copy-start.33 = (f32[1,128]{1,0:T(1,128)}, f32[1,128]{1,0:T(1,128)S(1)}, u32[]{:S(2)}) copy-start(f32[1,128]{1,0:T(1,128)S(1)} %get-tuple-element.113.dlog) | copy-start | bytes 1540
  18.4 87.7 %copy-start.35 = (f32[1,128]{1,0:T(1,128)}, f32[1,128]{1,0:T(1,128)S(1)}, u32[]{:S(2)}) copy-start(f32[1,128]{1,0:T(1,128)S(1)} %get-tuple-element.114.sbias) | copy-start | bytes 1540
  18.6 83.1 %copy-start.82 = (f32[256]{0:T(256)}, f32[256]{0:T(256)S(1)}, u32[]{:S(2)}) copy-start(f32[256]{0:T(256)S(1)} %add_rsqrt_fusion.2) | copy-start | bytes 3076
  101.6 4.4 collective-permute-start
  106.1 20.2 %copy-start.27 = (bf16[8,1792]{1,0:T(8,128)(2,1)}, bf16[8,1792]{1,0:T(8,128)(2,1)S(1)}, u32[]{:S(2)}) copy-start(bf16[8,1792]{1,0:T(8,128)(2,1)S(1)} %collective-permute-done.halo) | copy-start | bytes 86020
  110.2 150.6 %copy-start = (f32[256,1792]{1,0:T(8,128)}, f32[256,1792]{1,0:T(8,128)S(1)}, u32[]{:S(2)}) copy-start(f32[256,1792]{1,0:T(8,128)S(1)} %get-tuple-element.32.act) | copy-start | bytes 5505028
  112.0 16.6 %all-to-all-start = ((bf16[8,3,80,128]{3,2,1,0:T(8,128)(2,1)}), bf16[8,3,80,128]{3,2,1,0:T(8,128)(2,1)S(1)}, u32[]{:S(2)}, u32[]{:S(2)}) async-start(bf16[8,3,80,128]{3,2,1,0:T(8,128)(2,1)} %pad_maximum_fusion.3), calls=%async_computation | async-start | bytes 983040 | tf_op jit(solution)/shard_map/all_to_all | solution.py:413
  119.2 49.7 %copy-start.37 = (f32[1,128]{1,0:T(1,128)}, f32[1,128]{1,0:T(1,128)S(1)}, u32[]{:S(2)}) copy-start(f32[1,128]{1,0:T(1,128)S(1)} %pad_bitcast_fusion.skip) | copy-start | bytes 1540
  136.1 16.9 %all-to-all-start.1 = ((bf16[8,3,64,128]{3,2,1,0:T(8,128)(2,1)}), bf16[8,3,64,128]{3,2,1,0:T(8,128)(2,1)S(1)}, u32[]{:S(2)}, u32[]{:S(2)}) async-start(bf16[8,3,64,128]{3,2,1,0:T(8,128)(2,1)} %fusion.42), calls=%async_computation.1 | async-start | bytes 786432 | tf_op jit(solution)/shard_map/all_to_all | solution.py:422
  140.4 19.6 %copy-start.88 = (f32[16,64]{1,0:T(8,128)S(1)}, f32[16,64]{1,0:T(8,128)}, u32[]{:S(2)}) copy-start(f32[16,64]{1,0:T(8,128)} %get-tuple-element.84) | copy-start | bytes 12292
  154.1 31.6 %all-to-all-start.2 = ((bf16[8,256,256]{2,1,0:T(8,128)(2,1)}), bf16[8,256,256]{2,1,0:T(8,128)(2,1)}, u32[]{:S(2)}, u32[]{:S(2)}) async-start(bf16[8,256,256]{2,1,0:T(8,128)(2,1)} %broadcast_in_dim.25), calls=%async_computation.2 | async-start | bytes 2097152 | tf_op jit(solution)/shard_map/all_to_all | solution.py:319
  158.3 250.0 %reduce-scatter.3.cloned.1.call-start = ((), (), s32[]{:S(2)}) async-start(), calls=%async_computation.13 | async-start | bytes 17825792 | tf_op jit(solution)/shard_map/reduce_scatter | solution.py:492
  260.8 15.8 %copy-start.1 = (bf16[256,1536]{1,0:T(8,128)(2,1)}, bf16[256,1536]{1,0:T(8,128)(2,1)S(1)}, u32[]{:S(2)}) copy-start(bf16[256,1536]{1,0:T(8,128)(2,1)S(1)} %multiply_convert_fusion.3.gy) | copy-start | bytes 2359300
  282.0 14.7 %all-to-all-start.4 = ((bf16[8,3,64,128]{3,2,1,0:T(8,128)(2,1)}), bf16[8,3,64,128]{3,2,1,0:T(8,128)(2,1)}, u32[]{:S(2)}, u32[]{:S(2)}) async-start(bf16[8,3,64,128]{3,2,1,0:T(8,128)(2,1)} %constant_dynamic-update-slice_fusion.1), calls=%async_computation.4 | async-start | bytes 786432 | tf_op jit(solution)/shard_map/all_to_all | solution.py:503
  290.3 30.2 %copy-start.2 = (bf16[256,1536]{1,0:T(8,128)(2,1)S(1)}, bf16[256,1536]{1,0:T(8,128)(2,1)}, u32[]{:S(2)}) copy-start(bf16[256,1536]{1,0:T(8,128)(2,1)} %copy-done.1) | copy-start | bytes 2359300
  290.3 30.2 %copy-start.5 = (bf16[8,3,64,128]{3,2,1,0:T(8,128)(2,1)S(1)}, bf16[8,3,64,128]{3,2,1,0:T(8,128)(2,1)}, u32[]{:S(2)}) copy-start(bf16[8,3,64,128]{3,2,1,0:T(8,128)(2,1)} %copy-done.3) | copy-start | bytes 1179652
  290.3 30.2 %copy-start.18 = (f32[256,128]{1,0:T(8,128)S(1)}, f32[256,128]{1,0:T(8,128)}, u32[]{:S(2)}) copy-start(f32[256,128]{1,0:T(8,128)} %copy-done.15) | copy-start | bytes 393220
  296.7 58.6 %all-to-all-start.5 = ((bf16[8,256,256]{2,1,0:T(8,128)(2,1)}), bf16[8,256,256]{2,1,0:T(8,128)(2,1)}, u32[]{:S(2)}, u32[]{:S(2)}) async-start(bf16[8,256,256]{2,1,0:T(8,128)(2,1)} %bitcast.135), calls=%async_computation.5 | async-start | bytes 2097152 | tf_op jit(solution)/shard_map/all_to_all | solution.py:319
  320.2 207.2 %reduce-scatter.5.cloned.1.call-start = ((), (), s32[]{:S(2)}) async-start(), calls=%async_computation.14 | async-start | bytes 9191424 | tf_op jit(solution)/shard_map/reduce_scatter | solution.py:536
  325.7 19.0 %copy-start.50 = (f32[256,1536]{1,0:T(8,128)S(1)}, f32[256,1536]{1,0:T(8,128)}, u32[]{:S(2)}) copy-start(f32[256,1536]{1,0:T(8,128)} %copy-done.49) | copy-start | bytes 4718596
  325.7 19.0 %copy-start.78 = (f32[1536]{0:T(1024)S(1)}, f32[1536]{0:T(1024)}, u32[]{:S(2)}) copy-start(f32[1536]{0:T(1024)} %reshape.358) | copy-start | bytes 18436
  325.7 19.0 %copy-start.94 = (f32[256]{0:T(256)S(1)}, f32[256]{0:T(256)}, u32[]{:S(2)}) copy-start(f32[256]{0:T(256)} %add_rsqrt_fusion.1) | copy-start | bytes 3076
  325.7 19.0 %copy-start.96 = (f32[256]{0:T(256)S(1)}, f32[256]{0:T(256)}, u32[]{:S(2)}) copy-start(f32[256]{0:T(256)} %copy-done.95) | copy-start | bytes 3076
  343.3 8.1 %collective-permute-start.1 = (bf16[8,1792]{1,0:T(8,128)(2,1)S(1)}, bf16[8,1792]{1,0:T(8,128)(2,1)S(1)}, u32[]{:S(2)}, u32[]{:S(2)}) collective-permute-start(bf16[8,1792]{1,0:T(8,128)(2,1)S(1)} %slice.583), channel_id=1, source_target_pairs={{16,0},{32,16},{48,32},{64,48},{80,64},{96,80},{112,96},{17,1},{33... | collective-permute-start | bytes 86024 | tf_op jit(solution)/shard_map/ppermute | solution.py:522
  415.1 92.9 %all-to-all-start.8 = ((bf16[8,32,2048]{2,1,0:T(8,128)(2,1)}), bf16[8,32,2048]{2,1,0:T(8,128)(2,1)S(1)}, u32[]{:S(2)}, u32[]{:S(2)}) async-start(bf16[8,32,2048]{2,1,0:T(8,128)(2,1)} %bitcast.170), calls=%async_computation.10 | async-start | bytes 2097152 | tf_op jit(solution)/shard_map/all_to_all | solution.py:319
  509.2 15.6 %all-to-all-start.9 = ((bf16[8,32,2048]{2,1,0:T(8,128)(2,1)}), bf16[8,32,2048]{2,1,0:T(8,128)(2,1)S(1)}, u32[]{:S(2)}, u32[]{:S(2)}) async-start(bf16[8,32,2048]{2,1,0:T(8,128)(2,1)} %broadcast_in_dim.29), calls=%async_computation.11 | async-start | bytes 2097152 | tf_op jit(solution)/shard_map/all_to_all | solution.py:319
  527.4 12.3 %all-to-all-start.6 = ((bf16[8,8,4224]{2,1,0:T(8,128)(2,1)}), bf16[8,8,4224]{2,1,0:T(8,128)(2,1)S(1)}, u32[]{:S(2)}, u32[]{:S(2)}) async-start(bf16[8,8,4224]{2,1,0:T(8,128)(2,1)} %bitcast.171), calls=%async_computation.8 | async-start | bytes 1081344 | tf_op jit(solution)/shard_map/all_to_all | solution.py:319
  540.5 12.3 %all-to-all-start.7 = ((bf16[8,8,4224]{2,1,0:T(8,128)(2,1)}), bf16[8,8,4224]{2,1,0:T(8,128)(2,1)S(1)}, u32[]{:S(2)}, u32[]{:S(2)}) async-start(bf16[8,8,4224]{2,1,0:T(8,128)(2,1)} %broadcast_in_dim.28), calls=%async_computation.9 | async-start | bytes 1081344 | tf_op jit(solution)/shard_map/all_to_all | solution.py:319
  (99 other events, 549.9 us)
Sparse Core Ops, SparseCore 0:
  14.6 76.7 all-gather.3
  94.4 121.3 all-gather.5
  253.3 154.9 reduce-scatter.2
  412.5 102.2 reduce-scatter.4

commit v3 on v2

--- a/solution.py
+++ b/solution.py
@@ -296,6 +296,299 @@
     )(*args)
 
 
+def places():
+    s, f = lax.axis_index("seq"), lax.axis_index("fsdp")
+    return s // 2, s % 2, f // 4, (f // 2) % 2, f % 2
+
+
+def at_place(y, x_lo, z, x_hi, core):
+    return {"seq": y * 2 + x_lo, "fsdp": z * 4 + x_hi * 2 + core}
+
+
+def greet(others):
+    barrier = pltpu.get_barrier_semaphore()
+    for other in others:
+        pl.semaphore_signal(barrier, inc=1, device_id=other, device_id_type=pl.DeviceIdType.MESH)
+    pl.semaphore_wait(barrier, len(others))
+
+
+WIDTHS = (1024, 1024, 1024, 1152)
+
+
+def reduce_kernel(g, out, *refs):
+    n = len(WIDTHS)
+    groups = [refs[i * 10 : i * 10 + 10] for i in range(n)]
+    gathered, send, recv, local = refs[n * 10 :]
+    y, x_lo, z, x_hi, core = places()
+    yn, yp, yo = (y + 1) % 4, (y + 3) % 4, (y + 2) % 4
+    zn, zp, zo = (z + 1) % 4, (z + 3) % 4, (z + 2) % 4
+    y_next, y_prev = at_place(yn, x_lo, z, x_hi, core), at_place(yp, x_lo, z, x_hi, core)
+    y_far = at_place(yo, x_lo, z, x_hi, core)
+    z_next, z_prev = at_place(y, x_lo, zn, x_hi, core), at_place(y, x_lo, zp, x_hi, core)
+    across = at_place(y, 1 - x_lo, z, 1 - x_hi, core)
+    beside = at_place(y, 1 - x_lo, z, x_hi, core)
+    twin = at_place(y, x_lo, z, x_hi, 1 - core)
+    greet((y_next, y_prev, y_far, z_next, z_prev, across, beside, twin))
+
+    def copy(c, slot, source, target, device):
+        return pltpu.make_async_remote_copy(
+            src_ref=source, dst_ref=target, send_sem=send.at[c, slot], recv_sem=recv.at[c, slot],
+            device_id=device, device_id_type=pl.DeviceIdType.MESH,
+        )
+
+    started = []
+
+    def go(c, slot, source, target, device):
+        item = copy(c, slot, source, target, device)
+        item.start()
+        started.append(item)
+        return item
+
+    def lanes(c):
+        return pl.ds(sum(WIDTHS[:c]), WIDTHS[c])
+
+    first = [[None] * 16 for _ in range(n)]
+    loads = []
+    for c in range(n):
+        acc, twin_buf = groups[c][0], groups[c][1]
+        first[c][0] = go(c, 0, g.at[:, :, 1 - core, :, :, lanes(c)], twin_buf, twin)
+        load = pltpu.make_async_copy(g.at[:, :, core, :, :, lanes(c)], acc, local.at[c])
+        load.start()
+        loads.append(load)
+
+    def add(target, source):
+        target[...] = target[...] + source[...]
+
+    def stage(c, step):
+        acc, twin_buf, p1, m1, p2, m2, q1, r1, q2, r2 = groups[c][:10]
+        kept = first[c]
+        y_first = c % 2 == 0
+        if step == 0:
+            loads[c].wait()
+            kept[0].wait_recv()
+
+            def body(i, carry):
+                a, b, d = i // 8, (i // 4) % 2, i % 4
+                add(acc.at[a, b, d], twin_buf.at[a, b, d])
+                return carry
+
+            lax.fori_loop(0, 32, body, 0)
+            if y_first:
+                kept[1] = go(c, 1, acc.at[:, 0, yo], p1, y_next)
+                kept[2] = go(c, 2, acc.at[:, 1, yo], m1, y_prev)
+            else:
+                kept[1] = go(c, 1, acc.at[zo, 0], p1, z_next)
+                kept[2] = go(c, 2, acc.at[zo, 1], m1, z_prev)
+        elif step == 1:
+            kept[1].wait_recv()
+            kept[2].wait_recv()
+
+            def body(i, carry):
+                if y_first:
+                    add(acc.at[i, 0, yn], p1.at[i])
+                    add(acc.at[i, 1, yp], m1.at[i])
+                else:
+                    add(acc.at[zn, 0, i], p1.at[i])
+                    add(acc.at[zp, 1, i], m1.at[i])
+                return carry
+
+            lax.fori_loop(0, 4, body, 0)
+            if y_first:
+                kept[3] = go(c, 3, acc.at[:, :, yn], p2, y_next)
+                kept[4] = go(c, 4, acc.at[:, :, yp], m2, y_prev)
+            else:
+                kept[3] = go(c, 3, acc.at[zn], p2, z_next)
+                kept[4] = go(c, 4, acc.at[zp], m2, z_prev)
+        elif step == 2:
+            kept[3].wait_recv()
+            kept[4].wait_recv()
+
+            def body(i, carry):
+                if y_first:
+                    a, b = i // 2, i % 2
+                    add(acc.at[a, b, y], p2.at[a, b])
+                    add(acc.at[a, b, y], m2.at[a, b])
+                else:
+                    a, b = i // 4, i % 4
+                    add(acc.at[z, a, b], p2.at[a, b])
+                    add(acc.at[z, a, b], m2.at[a, b])
+                return carry
+
+            lax.fori_loop(0, 8, body, 0)
+            if y_first:
+                kept[5] = go(c, 5, acc.at[zo, 0, y], q1, z_next)
+                kept[6] = go(c, 6, acc.at[zo, 1, y], r1, z_prev)
+            else:
+                kept[5] = go(c, 5, acc.at[z, 0, yo], q1, y_next)
+                kept[6] = go(c, 6, acc.at[z, 1, yo], r1, y_prev)
+        elif step == 3:
+            kept[5].wait_recv()
+            kept[6].wait_recv()
+            if y_first:
+                add(acc.at[zn, 0, y], q1)
+                add(acc.at[zp, 1, y], r1)
+                kept[7] = go(c, 7, acc.at[zn, :, y], q2, z_next)
+                kept[8] = go(c, 8, acc.at[zp, :, y], r2, z_prev)
+            else:
+                add(acc.at[z, 0, yn], q1)
+                add(acc.at[z, 1, yp], r1)
+                kept[7] = go(c, 7, acc.at[z, :, yn], q2, y_next)
+                kept[8] = go(c, 8, acc.at[z, :, yp], r2, y_prev)
+        elif step == 4:
+            kept[7].wait_recv()
+            kept[8].wait_recv()
+            for b in range(2):
+                add(acc.at[z, b, y], q2.at[b])
+                add(acc.at[z, b, y], r2.at[b])
+            kept[9] = go(c, 9, acc.at[z, 1 - x_hi, y], gathered.at[4, :, lanes(c)], across)
+        elif step == 5:
+            kept[9].wait_recv()
+            acc[z, x_hi, y] = acc[z, x_hi, y] + gathered[4, :, lanes(c)]
+            kept[10] = go(c, 10, acc.at[z, x_hi, y], gathered.at[5, :, lanes(c)], beside)
+        elif step == 6:
+            kept[10].wait_recv()
+            gathered[y, :, lanes(c)] = acc[z, x_hi, y] + gathered[5, :, lanes(c)]
+            mine = gathered.at[y, :, lanes(c)]
+            kept[11] = go(c, 11, mine, mine, y_next)
+            kept[12] = go(c, 12, mine, mine, y_prev)
+            kept[13] = go(c, 13, mine, mine, y_far)
+        else:
+            for slot in (11, 12, 13):
+                kept[slot].wait_recv()
+
+    for step in range(8):
+        for c in range(n):
+            stage(c, step)
+    for i in range(4):
+        out[i] = gathered[i].astype(F32)
+    for item in started:
+        item.wait_send()
+
+
+def reduce_all(g):
+    cols = g.shape[1]
+    scratch = []
+    for c, w in enumerate(WIDTHS):
+        scratch += [pltpu.VMEM((4, 2, 4, 16, w), BF)] * 2 + [pltpu.VMEM((4, 16, w), BF)] * 2
+        scratch += [pltpu.VMEM((4, 2, 16, w) if c % 2 == 0 else (2, 4, 16, w), BF)] * 2
+        scratch += [pltpu.VMEM((16, w), BF)] * 2 + [pltpu.VMEM((2, 16, w), BF)] * 2
+    n = len(WIDTHS)
+    scratch += [
+        pltpu.VMEM((6, 16, cols), BF), pltpu.SemaphoreType.DMA((n, 14)), pltpu.SemaphoreType.DMA((n, 14)),
+        pltpu.SemaphoreType.DMA((n,)),
+    ]
+    out = pl.pallas_call(
+        reduce_kernel,
+        out_shape=jax.ShapeDtypeStruct((4, 16, cols), F32),
+        in_specs=[pl.BlockSpec(memory_space=pl.ANY)],
+        out_specs=pl.BlockSpec(memory_space=pltpu.VMEM),
+        scratch_shapes=scratch,
+        compiler_params=pltpu.CompilerParams(
+            collective_id=1, has_side_effects=True, vmem_limit_bytes=48 << 20
+        ),
+        cost_estimate=pl.CostEstimate(flops=10**8, bytes_accessed=10**8, transcendentals=0),
+    )(g.reshape(4, 2, 2, 4, 16, cols))
+    return out.reshape(64, cols)
+
+
+def gather_kernel(own, out, send, recv, local):
+    n = len(WIDTHS)
+    y, x_lo, z, x_hi, core = places()
+    yn, yp, yo = (y + 1) % 4, (y + 3) % 4, (y + 2) % 4
+    zn, zp, zo = (z + 1) % 4, (z + 3) % 4, (z + 2) % 4
+    y_next, y_prev = at_place(yn, x_lo, z, x_hi, core), at_place(yp, x_lo, z, x_hi, core)
+    z_next, z_prev = at_place(y, x_lo, zn, x_hi, core), at_place(y, x_lo, zp, x_hi, core)
+    across = at_place(y, 1 - x_lo, z, 1 - x_hi, core)
+    twin = at_place(y, x_lo, z, x_hi, 1 - core)
+    greet((y_next, y_prev, z_next, z_prev, across, twin))
+    started = []
+
+    def lanes(c):
+        return pl.ds(sum(WIDTHS[:c]), WIDTHS[c])
+
+    def go(c, slot, source, target, device):
+        item = pltpu.make_async_remote_copy(
+            src_ref=source, dst_ref=target, send_sem=send.at[c, slot], recv_sem=recv.at[c, slot],
+            device_id=device, device_id_type=pl.DeviceIdType.MESH,
+        )
+        item.start()
+        started.append(item)
+        return item
+
+    held = [[None] * 10 for _ in range(n)]
+    loads = []
+
+    def stage(c, step):
+        kept = held[c]
+        cols = lanes(c)
+        split = c % 2 == 0
+        rows = pl.ds(y, 1) if split else pl.ds(0, 4)
+
+        def part(a, b, d):
+            return out.at[a, b, core, d, :, cols]
+
+        def pass_on(slot, source, device):
+            kept[slot] = go(c, slot, source, source, device)
+
+        if step == 0:
+            kept[0] = go(c, 0, own.at[rows, :, cols], part(z, x_hi, rows), across)
+            load = pltpu.make_async_copy(own.at[rows, :, cols], part(z, x_hi, rows), local.at[c])
+            load.start()
+            loads.append(load)
+        elif step == 1:
+            loads[c].wait()
+            kept[0].wait_recv()
+            pass_on(1, part(z, slice(None), rows), z_next)
+            pass_on(2, part(z, slice(None), rows), z_prev)
+        elif step == 2:
+            kept[1].wait_recv()
+            kept[2].wait_recv()
+            pass_on(3, part(zp, 0, rows), z_next)
+            pass_on(4, part(zn, 1, rows), z_prev)
+        elif step == 3:
+            kept[3].wait_recv()
+            kept[4].wait_recv()
+            if split:
+                pass_on(5, part(slice(None), slice(None), rows), y_next)
+                pass_on(6, part(slice(None), slice(None), rows), y_prev)
+            else:
+                pass_on(9, part(slice(None), slice(None), rows), twin)
+        elif step == 4 and split:
+            kept[5].wait_recv()
+            kept[6].wait_recv()
+            pass_on(7, part(slice(None), 0, pl.ds(yp, 1)), y_next)
+            pass_on(8, part(slice(None), 1, pl.ds(yn, 1)), y_prev)
+        elif step == 5 and split:
+            kept[7].wait_recv()
+            kept[8].wait_recv()
+            pass_on(9, part(slice(None), slice(None), slice(None)), twin)
+        elif step == 6:
+            kept[9].wait_recv()
+
+    for step in range(7):
+        for c in range(n):
+            stage(c, step)
+    for item in started:
+        item.wait_send()
+
+
+def gather_all(own):
+    cols = own.shape[1]
+    n = len(WIDTHS)
+    out = pl.pallas_call(
+        gather_kernel,
+        out_shape=jax.ShapeDtypeStruct((4, 2, 2, 4, 16, cols), BF),
+        in_specs=[pl.BlockSpec(memory_space=pl.ANY)],
+        out_specs=pl.BlockSpec(memory_space=pl.ANY),
+        scratch_shapes=[
+            pltpu.SemaphoreType.DMA((n, 10)), pltpu.SemaphoreType.DMA((n, 10)), pltpu.SemaphoreType.DMA((n,))
+        ],
+        compiler_params=pltpu.CompilerParams(collective_id=2, has_side_effects=True),
+        cost_estimate=pl.CostEstimate(flops=10**8, bytes_accessed=10**8, transcendentals=0),
+    )(own.reshape(4, 16, cols))
+    return out.reshape(1024, cols)
+
+
 def rope_parts(length, start):
     half = AP // 2
     inverse = THETA ** (-2.0 * jnp.arange(half).astype(F32) / AP)
@@ -353,7 +646,7 @@
     front_shard = jnp.concatenate(
         [mixer_proj[:, : D_SSM + XBC], attn_proj, mixer_proj[:, D_SSM + XBC :], small], axis=1
     )
-    front = lax.all_gather(front_shard, "fsdp", axis=0, tiled=True)
+    front = gather_all(front_shard)
     tail_shard = jnp.concatenate(
         [
             gate_up[:, :FF],
@@ -362,7 +655,6 @@
         ],
         axis=0,
     )
-    tail_shard, _ = lax.optimization_barrier((tail_shard, front_shard))
     tail = lax.all_gather(tail_shard, "fsdp", axis=0, tiled=False)
     smalls = front.reshape(shards, width, FRONT)[:, :, 4120:].reshape(shards, slots)
     cuts = []
@@ -532,30 +824,23 @@
     grad_nin = dot(grad_proj, front, NT)
     grad_norm = jnp.sum(grad_nin * normed_one, axis=0)
     input_grad = grad_middle + rms_back(grad_nin * gain_one, normed_one, scale_one)
-    grad_front, tail_piece = lax.optimization_barrier((grad_front, tail_piece))
-    front_piece = lax.psum_scatter(grad_front, "fsdp", scatter_dimension=0, tiled=True)
-    front_sum, tail_sum = sum_over(front_piece, seqs), sum_over(tail_piece, seqs)
-    vectors = jnp.concatenate(
-        [
-            grad_norm, grad_ffn, grad_gated, dbias[0], dtaps[:4].reshape(-1),
-            dhead[0, :MH], dhead[1, :MH], dhead[2, :MH],
-        ]
-    )
-    vectors = lax.psum(vectors, ("seq", "fsdp"))
-    pos = lax.axis_index("fsdp")
-
-    def own(start, size, full):
-        return lax.dynamic_slice_in_dim(vectors[start : start + full], pos * size, size, 0)
-
+    vectors = [grad_norm, grad_ffn, grad_gated, dbias[0]] + [dtaps[lag] for lag in range(4)]
+    vectors = [value.reshape(shards, -1) for value in vectors]
+    vectors.append(jnp.broadcast_to(dhead[:3, :MH].reshape(1, 3 * MH), (shards, 3 * MH)))
+    vectors = jnp.concatenate(vectors, axis=1)
+    vectors = jnp.pad(vectors, ((0, 0), (0, slots - vectors.shape[1]))).astype(BF)
+    last = jnp.concatenate([grad_front[:, 4096:4120], vectors.reshape(-1, 104)], axis=1)
+    front_sum = reduce_all(lax.dynamic_update_slice(grad_front, last, (0, 4096)))
+    front_sum, tail_piece = lax.optimization_barrier((front_sum, tail_piece))
+    tail_sum = sum_over(tail_piece, seqs)
+    vectors = front_sum[:, 4120:].reshape(-1)
+    owned = []
     at = 0
-    owned = []
-    for size, full in ((width, 1024), (width, 1024), (gated_gain.shape[0], D_SSM), (kernel_size, XBC)):
-        owned.append(own(at, size, full))
-        at += full
-    own_taps = jnp.stack([own(at + lag * XBC, kernel_size, XBC) for lag in range(4)], axis=1)
-    at += 4 * XBC
+    for size in [width, width, gated_gain.shape[0], kernel_size] + [kernel_size] * 4 + [MH] * 3:
+        owned.append(vectors[at : at + size])
+        at += size
+    own_taps = jnp.stack(owned[4:8], axis=1)
     tail_sum = tail_sum.astype(F32)
-    front_sum = front_sum.astype(F32)
     return (
         block_out[None],
         input_grad[None],
@@ -564,9 +849,9 @@
         front_sum[:, 3328:4096],
         own_taps,
         owned[3],
-        vectors[at : at + MH],
-        vectors[at + MH : at + 2 * MH],
-        vectors[at + 2 * MH : at + 3 * MH],
+        owned[8],
+        owned[9],
+        owned[10],
         owned[2],
         tail_sum[low_rows : low_rows + mix_rows, :1024],
         tail_sum[low_rows + mix_rows :, :1024],

time: 570 us -> 489 us (0.86)
  waiting for transfers between devices: 185 us -> 54.5 us
  Pallas kernels: 35.6 us -> 162 us
  blocking collectives: 90.8 us -> 0 us
  starting transfers between devices: 62.2 us -> 75.7 us
  other arithmetic: 49.4 us -> 55.1 us
    pallas_call x0 -> x2, Pallas kernels: none -> 126 us  [the longest x1 67.4 us: gather_all(): pl.pallas_call(gather_kernel, out_shape=jax.ShapeDtypeStruct((4, 2, 2, 4,...]
    psum x1 -> x0, blocking collectives: 77 us -> none  [per_device(): vectors = lax.psum(vectors, ('seq', 'fsdp'))]
    all_gather x1 -> x0, waiting for transfers between devices: 72.8 us -> none  [per_device(): front = lax.all_gather(front_shard, 'fsdp', axis=0, tiled=True)]
    reduce_scatter x1, waiting for transfers between devices: 41.8 us -> 0.02 us  [per_device(): lax.psum_scatter(tail_grad, 'fsdp', scatter_dimension=0, tiled=True)[0]]
    all_to_all x6 -> x4, starting transfers between devices: 42.9 us -> 16.7 us  [exchange(): return lax.all_to_all(value, 'seq', split_axis=0, concat_axis=0, tiled=True)]
    all_gather x1, waiting for transfers between devices: 24.6 us -> 0.01 us  [per_device(): tail = lax.all_gather(tail_shard, 'fsdp', axis=0, tiled=False)]
    all_to_all x0 -> x1, starting transfers between devices: none -> 23.1 us  [per_device(): lax.all_to_all(dstart.reshape(seqs, heads, AP, NST), 'seq', split_axis=0,...]
    all_to_all x1, starting transfers between devices: 4.09 us -> 23.5 us  [per_device(): lax.all_to_all(jnp.stack(dends), 'seq', split_axis=0, concat_axis=0, tile...]
  transfers between devices with their start and end apart: 15 -> 12, of which waited for: 10 -> 6; matrix products, arithmetic and copies ran while one was open for 20% -> 23% of each run, Pallas kernels for 6% -> 34%
where the time goes in v3:
time: 489 us; the launch traced here: 480 us
  Pallas kernels  162 us (33%)
  starting transfers between devices  75.7 us (15%)
  local copies, waits for them, and re-layouts  69.7 us (14%)
  other arithmetic  55.1 us (11%)
  waiting for transfers between devices  54.5 us (11%)
  matrix products  47.3 us (10%)
  between operations  16.1 us (3%)
    pallas_call x1, Pallas kernels, gather_all(): pl.pallas_call(gather_kernel, out_shape=jax.ShapeDtypeStruct((4, 2, 2, 4,...  67.4 us
    pallas_call x1, Pallas kernels, reduce_all(): pl.pallas_call(reduce_kernel, out_shape=jax.ShapeDtypeStruct((4, 16, cols...  58.8 us
    dot_general x18, matrix products, dot(): lax.dot_general(a, b, dims, preferred_element_type=F32, precision=precision)  47.3 us
    pallas_call x6, Pallas kernels, call(): pl.pallas_call(kernel, out_shape=[jax.ShapeDtypeStruct(shape, dtype) for...  35.4 us
    all_to_all x1, starting transfers between devices, per_device(): lax.all_to_all(jnp.stack(dends), 'seq', split_axis=0, concat_axis=0, tile...  23.5 us
    all_to_all x1, starting transfers between devices, per_device(): lax.all_to_all(dstart.reshape(seqs, heads, AP, NST), 'seq', split_axis=0,...  23.1 us
    all_to_all x4, waiting for transfers between devices, exchange(): return lax.all_to_all(value, 'seq', split_axis=0, concat_axis=0, tiled=True)  23.1 us
    unnamed x17, other arithmetic  19.8 us
  transfers between devices with their start and end apart: 12, of which 6 were waited for; matrix products, arithmetic and copies ran while one was open for 23% of the time, Pallas kernels for 34%

profile of v3, /device:TPU:0, one launch (start us, length us, event | category | flops | bytes accessed | tf_op | source)
XLA Modules:
  0.0 479.9 jit_solution(14319479142586814567)
XLA Ops:
  11.9 67.4 %shard_map.279 = bf16[4,2,2,4,16,4224]{5,4,3,2,1,0:T(8,128)(2,1)} custom-call(bf16[4,16,4224]{2,1,0:T(8,128)(2,1)} %concatenate.75.own), custom_call_target="tpu_custom_call" | custom-call | flops 100000000 | bytes 100000000 | tf_op jit(solution)/shard_map/pallas_call | solution.py:578
  81.7 8.1 %fusion.69 = (bf16[256,4224]{1,0:T(8,128)(2,1)S(1)}, f32[256,4224]{1,0:T(8,128)}) fusion(bf16[1024,4224]{1,0:T(8,128)(2,1)} %bitcast.165, bf16[1,256,1024]{2,1,0:T(8,128)(2,1)S(1)} %copy-done.37, f32[1024]{0:T(1024)S(1)} %reshape.394, f32[256]{0:T(256)S(1)} %add_rsqrt_fusion.2), kind=kOutput, calls=%fused_computation.190 | convolution fusion | flops 2216722432 | bytes 15668224 | tf_op jit(solution)/shard_map/dot_general | solution.py:31
  98.0 3.4 shard_map.280
  103.9 4.9 %all-to-all-start = ((bf16[8,3,80,128]{3,2,1,0:T(8,128)(2,1)}), bf16[8,3,80,128]{3,2,1,0:T(8,128)(2,1)S(1)}, u32[]{:S(2)}, u32[]{:S(2)}) async-start(bf16[8,3,80,128]{3,2,1,0:T(8,128)(2,1)} %pad_maximum_fusion.3), calls=%async_computation | async-start | bytes 983040 | tf_op jit(solution)/shard_map/all_to_all | solution.py:705
  111.6 12.3 %all-to-all-done = bf16[8,3,80,128]{3,2,1,0:T(8,128)(2,1)S(1)} async-done(((bf16[8,3,80,128]{3,2,1,0:T(8,128)(2,1)}), bf16[8,3,80,128]{3,2,1,0:T(8,128)(2,1)S(1)}, u32[]{:S(2)}, u32[]{:S(2)}) %all-to-all-start) | async-done | bytes 491552 | tf_op jit(solution)/shard_map/all_to_all | solution.py:705
  129.7 3.5 all-to-all-start.1
  135.1 6.9 %all-to-all-done.1 = bf16[8,3,64,128]{3,2,1,0:T(8,128)(2,1)S(1)} async-done(((bf16[8,3,64,128]{3,2,1,0:T(8,128)(2,1)}), bf16[8,3,64,128]{3,2,1,0:T(8,128)(2,1)S(1)}, u32[]{:S(2)}, u32[]{:S(2)}) %all-to-all-start.1) | async-done | bytes 393248 | tf_op jit(solution)/shard_map/all_to_all | solution.py:714
  143.1 4.4 all-to-all-start.2
  165.9 4.6 shard_map.281
  173.9 3.8 shard_map.282
  182.5 3.9 slice.418
  186.4 5.7 %fusion.62 = (bf16[16,64,2048]{2,1,0:T(8,128)(2,1)S(1)}, bf16[16,64,2048]{2,1,0:T(8,128)(2,1)S(1)}) fusion(bf16[16,256,2048]{2,1,0:T(8,128)(2,1)} %bitcast.176), kind=kLoop, calls=%fused_computation.183 | loop fusion | bytes 16777216 | tf_op jit(solution)/shard_map/slice | solution.py:725
  209.6 6.8 %maximum_maximum_fusion = bf16[16,256,2048]{2,1,0:T(8,128)(2,1)} fusion(bf16[16,128,1024]{2,1,0:T(8,128)(2,1)S(1)} %bitcast.168, bf16[16,32,1024]{2,1,0:T(8,128)(2,1)S(1)} %bitcast.184, bf16[16,96,1024]{2,1,0:T(8,128)(2,1)S(1)} %bitcast.189, bf16[16,64,2048]{2,1,0:T(8,128)(2,1)S(1)} %bitcast.169, bf16[16,64,2048]{2,1,0:T(8,128)(2,1)S(1)} %bitcast.170), kind=kLoop, calls=%fused_computation | loop fusion | flops 83886080 | bytes 33554432 | tf_op jit(solution)/shard_map/concatenate | solution.py:764
  223.2 4.6 multiply_reduce_fusion
  233.8 23.1 %all-to-all-start.3 = ((bf16[8,3,64,128]{3,2,1,0:T(8,128)(2,1)}), bf16[8,3,64,128]{3,2,1,0:T(8,128)(2,1)}, u32[]{:S(2)}, u32[]{:S(2)}) async-start(bf16[8,3,64,128]{3,2,1,0:T(8,128)(2,1)} %bitcast.161), calls=%async_computation.3 | async-start | bytes 786432 | tf_op jit(solution)/shard_map/all_to_all | solution.py:787
  256.9 4.7 fusion.33
  263.5 4.5 shard_map.285
  276.8 23.5 %all-to-all-start.4 = ((bf16[8,3,64,128]{3,2,1,0:T(8,128)(2,1)}), bf16[8,3,64,128]{3,2,1,0:T(8,128)(2,1)S(1)}, u32[]{:S(2)}, u32[]{:S(2)}) async-start(bf16[8,3,64,128]{3,2,1,0:T(8,128)(2,1)} %constant_dynamic-update-slice_fusion.1), calls=%async_computation.4 | async-start | bytes 786432 | tf_op jit(solution)/shard_map/all_to_all | solution.py:795
  300.3 4.8 %fusion.21 = bf16[1,256,1024]{2,1,0:T(8,128)(2,1)} fusion(f32[256,1024]{1,0:T(8,128)S(1)} %copy-done.35, bf16[256,2048]{1,0:T(8,128)(2,1)} %copy-done.53, bf16[2048,1024]{1,0:T(8,128)(2,1)} %bitcast.186), kind=kOutput, calls=%fused_computation.50 | convolution fusion | flops 1074266112 | bytes 6815744 | tf_op jit(solution)/shard_map/dot_general | solution.py:31
  305.2 8.3 %all-to-all-done.4 = bf16[8,3,64,128]{3,2,1,0:T(8,128)(2,1)S(1)} async-done(((bf16[8,3,64,128]{3,2,1,0:T(8,128)(2,1)}), bf16[8,3,64,128]{3,2,1,0:T(8,128)(2,1)S(1)}, u32[]{:S(2)}, u32[]{:S(2)}) %all-to-all-start.4) | async-done | bytes 393248 | tf_op jit(solution)/shard_map/all_to_all | solution.py:795
  313.5 4.4 all-to-all-start.5
  318.1 17.3 %shard_map.284 = (f32[256,1792]{1,0:T(8,128)S(1)}, f32[8,1792]{1,0:T(8,128)S(1)}, f32[8,1792]{1,0:T(8,128)S(1)}, bf16[256,128]{1,0:T(8,128)(2,1)S(1)}, f32[8,128]{1,0:T(8,128)S(1)}) custom-call(bf16[256,1536]{1,0:T(8,128)(2,1)S(1)} %copy-done.2, bf16[256,1792]{1,0:T(8,128)(2,1)S(1)} %slice.386.xbc, bf16[8,1792]{1,0:T(8,128)(2,1)S(1)} %copy-done.26, ...), custom_call_target="tpu_custom_call" | custom-call | tf_op jit(solution)/shard_map/pallas_call | solution.py:289
  338.5 3.9 collective-permute-done.1
  342.5 5.3 %fusion.32 = bf16[256,4224]{1,0:T(8,128)(2,1)} fusion(bf16[256,4224]{1,0:T(8,128)(2,1)} %fusion.33, f32[8,1792]{1,0:T(8,128)S(1)} %convert_element_type.349, f32[256,1792]{1,0:T(8,128)} %copy-done.11, f32[1792]{0:T(1024)S(1)} %copy-done.79, f32[1792]{0:T(1024)S(1)} %copy-done.80, f32[1792]{0:T(1024)S(1)} %copy-done.81, f32[1792]{0:T(1024)S(1)} %copy-done.78), kind=kLoop, calls=%fused_computation.69 | loop fusion | flops 5046272 | bytes 2838528
  352.4 7.7 %fusion.28 = (bf16[1024]{0:T(1024)(128)(2,1)S(1)}, f32[256]{0:T(256)S(1)}, f32[256,1024]{1,0:T(8,128)}) fusion(bf16[1,256,1024]{2,1,0:T(8,128)(2,1)S(1)} %copy-done.39, f32[256]{0:T(256)S(1)} %copy-done.77, f32[1024]{0:T(1024)S(1)} %copy-done.64, bf16[256,4224]{1,0:T(8,128)(2,1)} %constant_dynamic-update-slice_fusion.2, bf16[1024,4224]{1,0:T(8,128)(2,1)} %bitcast.166), kind=kOutput, calls=%fused_computation.58 | convolution fusion | flops 2216426240 | bytes 12394496 | tf_op jit(solution)/shard_map/dot_general | solution.py:31
  360.9 4.2 convolution_convert_fusion
  365.4 3.6 copy-done.33
  369.0 58.8 %shard_map.286 = f32[4,16,4224]{2,1,0:T(8,128)S(1)} custom-call(bf16[4,2,2,4,16,4224]{5,4,3,2,1,0:T(8,128)(2,1)} %bitcast.167), custom_call_target="tpu_custom_call" | custom-call | flops 100000000 | bytes 100000000 | tf_op jit(solution)/shard_map/pallas_call | solution.py:480
  427.8 4.4 all-to-all-start.6
  437.9 10.2 %all-to-all-done.6 = bf16[8,32,2048]{2,1,0:T(8,128)(2,1)} async-done(((bf16[8,32,2048]{2,1,0:T(8,128)(2,1)}), bf16[8,32,2048]{2,1,0:T(8,128)(2,1)}, u32[]{:S(2)}, u32[]{:S(2)}) %all-to-all-start.6) | async-done | bytes 1048608 | tf_op jit(solution)/shard_map/all_to_all | solution.py:612
  450.6 3.6 all-to-all-start.7
  456.4 12.8 %all-to-all-done.7 = bf16[8,32,2048]{2,1,0:T(8,128)(2,1)S(1)} async-done(((bf16[8,32,2048]{2,1,0:T(8,128)(2,1)}), bf16[8,32,2048]{2,1,0:T(8,128)(2,1)S(1)}, u32[]{:S(2)}, u32[]{:S(2)}) %all-to-all-start.7) | async-done | bytes 1048608 | tf_op jit(solution)/shard_map/all_to_all | solution.py:612
  (406 shorter events, 118.7 us)
Async XLA Ops:
  7.2 171.3 %all-gather.3.cloned.1.call-start = ((), (), s32[]{:S(2)}) async-start(), calls=%async_computation.10 | async-start | bytes 17825792 | tf_op jit(solution)/shard_map/all_gather | solution.py:658
  11.9 69.6 %copy-start.37 = (bf16[1,256,1024]{2,1,0:T(8,128)(2,1)S(1)}, bf16[1,256,1024]{2,1,0:T(8,128)(2,1)}, u32[]{:S(2)}) copy-start(bf16[1,256,1024]{2,1,0:T(8,128)(2,1)} %param.16) | copy-start | bytes 1572868
  80.7 13.3 %copy-start.66 = (bf16[16,6656]{1,0:T(8,128)(2,1)}, bf16[16,6656]{1,0:T(8,128)(2,1)S(1)}, u32[]{:S(2)}) copy-start(bf16[16,6656]{1,0:T(8,128)(2,1)S(1)} %reshape.360) | copy-start | bytes 638980
  81.6 13.1 %copy-start.109 = (f32[24]{0:T(128)S(1)}, f32[24]{0:T(128)}, u32[]{:S(2)}) copy-start(f32[24]{0:T(128)} %param.23) | copy-start | bytes 292
  81.7 13.0 %copy-start.110 = (f32[24]{0:T(128)S(1)}, f32[24]{0:T(128)}, u32[]{:S(2)}) copy-start(f32[24]{0:T(128)} %param.22) | copy-start | bytes 292
  90.4 7.5 %collective-permute-start = (bf16[8,1792]{1,0:T(8,128)(2,1)}, bf16[8,1792]{1,0:T(8,128)(2,1)S(1)}, u32[]{:S(2)}, u32[]{:S(2)}) collective-permute-start(bf16[8,1792]{1,0:T(8,128)(2,1)} %slice.387), channel_id=1, source_target_pairs={{0,16},{16,32},{32,48},{48,64},{64,80},{80,96},{96,112},{1,17},{17... | collective-permute-start | bytes 86024 | tf_op jit(solution)/shard_map/ppermute | solution.py:689
  96.1 13.9 %copy-start.55 = (f32[256,128]{1,0:T(8,128)}, f32[256,128]{1,0:T(8,128)S(1)}, u32[]{:S(2)}) copy-start(f32[256,128]{1,0:T(8,128)S(1)} %copy.88) | copy-start | bytes 393220
  96.2 13.8 %copy-start.57 = (f32[256,128]{1,0:T(8,128)}, f32[256,128]{1,0:T(8,128)S(1)}, u32[]{:S(2)}) copy-start(f32[256,128]{1,0:T(8,128)S(1)} %copy.91) | copy-start | bytes 393220
  97.9 26.8 %copy-start.25 = (bf16[8,1792]{1,0:T(8,128)(2,1)}, bf16[8,1792]{1,0:T(8,128)(2,1)S(1)}, u32[]{:S(2)}) copy-start(bf16[8,1792]{1,0:T(8,128)(2,1)S(1)} %collective-permute-done.halo) | copy-start | bytes 86020
  102.1 129.1 %copy-start = (f32[256,1792]{1,0:T(8,128)}, f32[256,1792]{1,0:T(8,128)S(1)}, u32[]{:S(2)}) copy-start(f32[256,1792]{1,0:T(8,128)S(1)} %get-tuple-element.31.act) | copy-start | bytes 5505028
  103.9 20.1 %all-to-all-start = ((bf16[8,3,80,128]{3,2,1,0:T(8,128)(2,1)}), bf16[8,3,80,128]{3,2,1,0:T(8,128)(2,1)S(1)}, u32[]{:S(2)}, u32[]{:S(2)}) async-start(bf16[8,3,80,128]{3,2,1,0:T(8,128)(2,1)} %pad_maximum_fusion.3), calls=%async_computation | async-start | bytes 983040 | tf_op jit(solution)/shard_map/all_to_all | solution.py:705
  111.6 21.5 %copy-start.67 = (bf16[256,128]{1,0:T(8,128)(2,1)S(1)}, bf16[256,128]{1,0:T(8,128)(2,1)}, u32[]{:S(2)}) copy-start(bf16[256,128]{1,0:T(8,128)(2,1)} %get-tuple-element.80) | copy-start | bytes 196612
  111.6 21.6 %copy-start.68 = (bf16[256,128]{1,0:T(8,128)(2,1)S(1)}, bf16[256,128]{1,0:T(8,128)(2,1)}, u32[]{:S(2)}) copy-start(bf16[256,128]{1,0:T(8,128)(2,1)} %add_convert_fusion.1) | copy-start | bytes 196612
  129.7 12.3 %all-to-all-start.1 = ((bf16[8,3,64,128]{3,2,1,0:T(8,128)(2,1)}), bf16[8,3,64,128]{3,2,1,0:T(8,128)(2,1)S(1)}, u32[]{:S(2)}, u32[]{:S(2)}) async-start(bf16[8,3,64,128]{3,2,1,0:T(8,128)(2,1)} %fusion.52), calls=%async_computation.1 | async-start | bytes 786432 | tf_op jit(solution)/shard_map/all_to_all | solution.py:714
  133.2 14.5 %copy-start.111 = (f32[24]{0:T(128)S(1)}, f32[24]{0:T(128)}, u32[]{:S(2)}) copy-start(f32[24]{0:T(128)} %param.24) | copy-start | bytes 292
  133.2 14.5 %copy-start.62 = (f32[256,64]{0,1:T(8,128)S(1)}, f32[256,64]{0,1:T(8,128)}, u32[]{:S(2)}) copy-start(f32[256,64]{0,1:T(8,128)} %copy-done.61) | copy-start | bytes 196612
  143.1 29.9 %all-to-all-start.2 = ((bf16[8,256,256]{2,1,0:T(8,128)(2,1)}), bf16[8,256,256]{2,1,0:T(8,128)(2,1)}, u32[]{:S(2)}, u32[]{:S(2)}) async-start(bf16[8,256,256]{2,1,0:T(8,128)(2,1)} %broadcast_in_dim.27), calls=%async_computation.2 | async-start | bytes 2097152 | tf_op jit(solution)/shard_map/all_to_all | solution.py:612
  147.5 280.3 %reduce-scatter.2.cloned.1.call-start = ((), (), s32[]{:S(2)}) async-start(), calls=%async_computation.9 | async-start | bytes 17825792 | tf_op jit(solution)/shard_map/reduce_scatter | solution.py:784
  147.7 15.3 %copy-start.31 = (f32[1,128]{1,0:T(1,128)}, f32[1,128]{1,0:T(1,128)S(1)}, u32[]{:S(2)}) copy-start(f32[1,128]{1,0:T(1,128)S(1)} %pad_bitcast_fusion.skip) | copy-start | bytes 1540
  179.8 14.1 %copy-start.40 = (bf16[16,32,1024]{2,1,0:T(8,128)(2,1)}, bf16[16,32,1024]{2,1,0:T(8,128)(2,1)S(1)}, u32[]{:S(2)}) copy-start(bf16[16,32,1024]{2,1,0:T(8,128)(2,1)S(1)} %slice.414) | copy-start | bytes 3145732
  233.8 36.5 %all-to-all-start.3 = ((bf16[8,3,64,128]{3,2,1,0:T(8,128)(2,1)}), bf16[8,3,64,128]{3,2,1,0:T(8,128)(2,1)}, u32[]{:S(2)}, u32[]{:S(2)}) async-start(bf16[8,3,64,128]{3,2,1,0:T(8,128)(2,1)} %bitcast.161), calls=%async_computation.3 | async-start | bytes 786432 | tf_op jit(solution)/shard_map/all_to_all | solution.py:787
  270.3 30.0 %copy-start.35 = (f32[256,1024]{1,0:T(8,128)S(1)}, f32[256,1024]{1,0:T(8,128)}, u32[]{:S(2)}) copy-start(f32[256,1024]{1,0:T(8,128)} %copy-done.34) | copy-start | bytes 3145732
  276.8 36.7 %all-to-all-start.4 = ((bf16[8,3,64,128]{3,2,1,0:T(8,128)(2,1)}), bf16[8,3,64,128]{3,2,1,0:T(8,128)(2,1)S(1)}, u32[]{:S(2)}, u32[]{:S(2)}) async-start(bf16[8,3,64,128]{3,2,1,0:T(8,128)(2,1)} %constant_dynamic-update-slice_fusion.1), calls=%async_computation.4 | async-start | bytes 786432 | tf_op jit(solution)/shard_map/all_to_all | solution.py:795
  305.1 12.8 %copy-start.22 = (f32[256,128]{1,0:T(8,128)S(1)}, f32[256,128]{1,0:T(8,128)}, u32[]{:S(2)}) copy-start(f32[256,128]{1,0:T(8,128)} %copy-done.20) | copy-start | bytes 393220
  313.5 35.2 %all-to-all-start.5 = ((bf16[8,256,256]{2,1,0:T(8,128)(2,1)}), bf16[8,256,256]{2,1,0:T(8,128)(2,1)}, u32[]{:S(2)}, u32[]{:S(2)}) async-start(bf16[8,256,256]{2,1,0:T(8,128)(2,1)} %bitcast.162), calls=%async_computation.5 | async-start | bytes 2097152 | tf_op jit(solution)/shard_map/all_to_all | solution.py:612
  318.0 24.4 %copy-start.78 = (f32[1792]{0:T(1024)S(1)}, f32[1792]{0:T(1024)}, u32[]{:S(2)}) copy-start(f32[1792]{0:T(1024)} %mul.488) | copy-start | bytes 21508
  318.0 24.4 %copy-start.79 = (f32[1792]{0:T(1024)S(1)}, f32[1792]{0:T(1024)}, u32[]{:S(2)}) copy-start(f32[1792]{0:T(1024)} %mul.505) | copy-start | bytes 21508
  318.0 24.4 %copy-start.80 = (f32[1792]{0:T(1024)S(1)}, f32[1792]{0:T(1024)}, u32[]{:S(2)}) copy-start(f32[1792]{0:T(1024)} %mul.502) | copy-start | bytes 21508
  318.1 24.4 %copy-start.81 = (f32[1792]{0:T(1024)S(1)}, f32[1792]{0:T(1024)}, u32[]{:S(2)}) copy-start(f32[1792]{0:T(1024)} %mul.499) | copy-start | bytes 21508
  336.6 5.9 %collective-permute-start.1 = (bf16[8,1792]{1,0:T(8,128)(2,1)S(1)}, bf16[8,1792]{1,0:T(8,128)(2,1)S(1)}, u32[]{:S(2)}, u32[]{:S(2)}) collective-permute-start(bf16[8,1792]{1,0:T(8,128)(2,1)S(1)} %slice.611), channel_id=1, source_target_pairs={{16,0},{32,16},{48,32},{64,48},{80,64},{96,80},{112,96},{17,1},{33... | collective-permute-start | bytes 86024 | tf_op jit(solution)/shard_map/ppermute | solution.py:814
  427.8 20.3 %all-to-all-start.6 = ((bf16[8,32,2048]{2,1,0:T(8,128)(2,1)}), bf16[8,32,2048]{2,1,0:T(8,128)(2,1)}, u32[]{:S(2)}, u32[]{:S(2)}) async-start(bf16[8,32,2048]{2,1,0:T(8,128)(2,1)} %bitcast.202), calls=%async_computation.7 | async-start | bytes 2097152 | tf_op jit(solution)/shard_map/all_to_all | solution.py:612
  450.6 18.5 %all-to-all-start.7 = ((bf16[8,32,2048]{2,1,0:T(8,128)(2,1)}), bf16[8,32,2048]{2,1,0:T(8,128)(2,1)S(1)}, u32[]{:S(2)}, u32[]{:S(2)}) async-start(bf16[8,32,2048]{2,1,0:T(8,128)(2,1)} %broadcast_in_dim.61), calls=%async_computation.8 | async-start | bytes 2097152 | tf_op jit(solution)/shard_map/all_to_all | solution.py:612
  (96 other events, 523.6 us)
Sparse Core Ops, SparseCore 0:
  11.1 130.7 all-gather.2
  216.5 185.5 reduce-scatter.1
